TPU v7x, 32 devices: a whole 2x2x4 slice. The times are simulated.
32 devices in a mesh: groups: 2 (over y), req: 16 (over z, x, core).
Axes of the slice: x: 2, y: 2, z: 4, core: 2. Of those that a mesh axis runs over, the one named last changes fastest.
Arguments:
- kv_cache: bfloat16 [1152, 2, 128, 512], P(('groups', 'req')), parts along dimension 0
- draft_rows: bfloat16 [1536, 5120], P(('groups', 'req')), parts along dimension 0
- cache_lengths: int32 [384], P('groups'), parts along dimension 0, may hold values from 1 to 384, as said below
- row_offsets: int32 [32], P('groups'), parts along dimension 0, may hold values from 0 to 15, as said below
- draft_order: int32 [1536], P(('groups', 'req')), parts along dimension 0, may hold values from 0 to 47, as said below
- pair_mask: int32 [2], P('groups'), parts along dimension 0, may hold values from 1 to 15
- moved_slots: int32 [32], P('groups'), parts along dimension 0, may hold values from 0 to 11
Outputs:
- verified: bfloat16 [1536, 4096], P(('groups', 'req')), parts along dimension 0
There are 2 independent parts, one for each index of `groups`. A program takes and returns all parts, laid end to end along the dimension named above; each array names one. Nothing has to cross between parts.
Inputs may be any that keep to these rules, and one draw needn't show every extreme that they name: `row_offsets`: all entries are different; the offsets 1, 15 and 8 are always among them. `draft_order`: each device's 48 entries are a permutation. `cache_lengths`: some request has exactly 384 positions.
All inputs are finite; a program needn't handle non-finite values.
Results may differ from a plain program's by a relative error of at most 0.0037.
Values may be sent and summed in bfloat16 or wider, within the bound.
No kernel may reach another device: no remote copies, remote signals or barrier semaphores. Data moves between devices by JAX's collectives and lax.ppermute only.
A program may use at most 128 MiB of HBM per device.

v0:
```python
import jax
import jax.numpy as jnp
from jax import lax
from jax.sharding import PartitionSpec as P

QH = 32
KVH = 4
HD = 128
DRAFT = 4
PAGE = 128
R_DEV = 12
PPR = 3
QW = 4096
KVW = 512


def from_partner(value, axis, apart):
    return lax.ppermute(value, axis, [(i, i ^ 1 << apart) for i in range(lax.axis_size(axis))])


def attend_slots(page_pool, lengths, row_block):
    grp = QH // KVH
    slots = page_pool.shape[0]
    span = page_pool.shape[1] * page_pool.shape[3]
    cache_keys = page_pool[:, :, 0].reshape(slots, span, KVH, HD)
    cache_vals = page_pool[:, :, 1].reshape(slots, span, KVH, HD)
    queries = row_block[:, :, :QW].reshape(slots, DRAFT, KVH, grp, HD)
    new_keys = row_block[:, :, QW : QW + KVW].reshape(slots, DRAFT, KVH, HD)
    new_vals = row_block[:, :, QW + KVW :].reshape(slots, DRAFT, KVH, HD)
    factor = 1.0 / jnp.sqrt(jnp.float32(HD))
    cache_score = (
        jnp.einsum("rtghd,rlgd->rtghl", queries, cache_keys, preferred_element_type=jnp.float32)
        * factor
    )
    new_score = (
        jnp.einsum("rtghd,rugd->rtghu", queries, new_keys, preferred_element_type=jnp.float32)
        * factor
    )
    cache_valid = (jnp.arange(span, dtype=jnp.int32)[None, :] < lengths[:, None])[
        :, None, None, None, :
    ]
    positions = jnp.arange(DRAFT, dtype=jnp.int32)
    new_valid = (positions[None, :] <= positions[:, None])[None, :, None, None, :]
    cache_score = jnp.where(cache_valid, cache_score, jnp.float32(-1e30))
    new_score = jnp.where(new_valid, new_score, jnp.float32(-1e30))
    peak = jnp.maximum(jnp.max(cache_score, axis=-1), jnp.max(new_score, axis=-1))
    cache_weight = jnp.where(cache_valid, jnp.exp(cache_score - peak[..., None]), 0.0)
    new_weight = jnp.where(new_valid, jnp.exp(new_score - peak[..., None]), 0.0)
    denominator = jnp.sum(cache_weight, axis=-1) + jnp.sum(new_weight, axis=-1)
    summed = jnp.einsum(
        "rtghl,rlgd->rtghd",
        cache_weight.astype(jnp.bfloat16),
        cache_vals,
        preferred_element_type=jnp.float32,
    )
    summed = summed + jnp.einsum(
        "rtghu,rugd->rtghd",
        new_weight.astype(jnp.bfloat16),
        new_vals,
        preferred_element_type=jnp.float32,
    )
    return (summed / denominator[..., None]).reshape(slots, DRAFT, QW).astype(jnp.bfloat16)


def on_device(
    kv_cache, draft_rows, cache_lengths, row_offsets, draft_order, pair_mask, moved_slots
):
    count = lax.axis_size("req")
    own_index = lax.axis_index("req")
    sections = count.bit_length() - 1
    rows_here = draft_rows.shape[0]
    per_peer = max(1, rows_here // count)
    slot_total = count * per_peer
    place_ids = jnp.arange(slot_total, dtype=jnp.int32)
    targets = (own_index - row_offsets[draft_order // per_peer]) % count
    send_place = targets * per_peer + draft_order % per_peer
    send_map = (place_ids[:, None] == send_place[None, :]).astype(jnp.bfloat16)
    outgoing = jnp.dot(send_map, draft_rows, preferred_element_type=jnp.float32).astype(
        jnp.bfloat16
    )
    incoming = lax.all_to_all(outgoing, "req", split_axis=0, concat_axis=0, tiled=True)
    owner_rows = jnp.arange(rows_here, dtype=jnp.int32)
    sources = (own_index + row_offsets[owner_rows // per_peer]) % count
    recv_place = sources * per_peer + owner_rows % per_peer
    recv_map = (recv_place[:, None] == place_ids[None, :]).astype(jnp.bfloat16)
    owned = jnp.dot(recv_map, incoming, preferred_element_type=jnp.float32).astype(jnp.bfloat16)
    owned = owned.reshape(R_DEV, DRAFT, owned.shape[-1])
    my_slot = moved_slots[own_index]
    page_pool = kv_cache.reshape(R_DEV, PPR, 2, PAGE, kv_cache.shape[-1])
    visitor = lax.dynamic_index_in_dim(owned, my_slot, 0, keepdims=False)
    for section in range(sections):
        arrived = from_partner(visitor, "req", section)
        visitor = jnp.where(
            jnp.bitwise_and(jnp.right_shift(pair_mask[0], section), 1) == 1, arrived, visitor
        )
    queries = lax.dynamic_update_index_in_dim(owned, visitor, my_slot, 0)
    lengths = lax.dynamic_slice_in_dim(cache_lengths, own_index * R_DEV, R_DEV)
    results = attend_slots(page_pool, lengths, queries)
    answer = lax.dynamic_index_in_dim(results, my_slot, 0, keepdims=False)
    for section in range(sections):
        arrived = from_partner(answer, "req", section)
        answer = jnp.where(
            jnp.bitwise_and(jnp.right_shift(pair_mask[0], section), 1) == 1, arrived, answer
        )
    results = lax.dynamic_update_index_in_dim(results, answer, my_slot, 0)
    flat_results = results.reshape(R_DEV * DRAFT, results.shape[-1])
    backward = jnp.dot(recv_map.T, flat_results, preferred_element_type=jnp.float32).astype(
        jnp.bfloat16
    )
    returned = lax.all_to_all(backward, "req", split_axis=0, concat_axis=0, tiled=True)
    return jnp.dot(send_map.T, returned, preferred_element_type=jnp.float32).astype(jnp.bfloat16)


def solution(mesh):
    in_specs = (
        P(("groups", "req"), None, None, None),
        P(("groups", "req"), None),
        P("groups"),
        P("groups"),
        P(("groups", "req")),
        P("groups"),
        P("groups"),
    )
    out_specs = P(("groups", "req"), None)
    return jax.shard_map(
        on_device, mesh=mesh, in_specs=in_specs, out_specs=out_specs, check_vma=False
    )
```

profile of v0, /device:TPU:0, one launch (start us, length us, event | category | flops | bytes accessed | tf_op | source)
XLA Modules:
  0.0 106.8 jit_solution(16687061333840150898)
XLA Ops:
  0.0 0.0 copy-start
  0.0 0.0 copy-start.1
  0.0 0.0 copy-start.3
  0.0 0.7 compare_select_fusion.1
  0.7 1.4 %gather_fusion = s32[48]{0:T(128)S(1)} fusion(s32[16]{0:T(128)} %param.10, s32[1024]{0:T(1024)S(1)} %pad_clamp_fusion.1), kind=kCustom, calls=%fused_computation | custom fusion | bytes 576 | tf_op jit(solution)/shard_map/gather | solution.py:75
  2.2 0.7 fusion.35
  2.9 0.0 copy-done
  2.9 0.3 convolution_convert_fusion.1
  3.1 1.1 %all_to_all.16 = bf16[16,3,5120]{2,1,0:T(4,128)(2,1)} reshape(bf16[48,5120]{1,0:T(8,128)(2,1)S(1)} %convolution_convert_fusion.1) | data formatting | bytes 983040 | tf_op jit(solution)/shard_map/all_to_all | solution.py:81
  4.3 7.4 %all-to-all-start = ((bf16[16,3,5120]{2,1,0:T(4,128)(2,1)}), bf16[16,3,5120]{2,1,0:T(4,128)(2,1)S(1)}, u32[]{:S(2)}, u32[]{:S(2)}) async-start(bf16[16,3,5120]{2,1,0:T(4,128)(2,1)} %all_to_all.16), calls=%async_computation | async-start | bytes 1310720 | tf_op jit(solution)/shard_map/all_to_all | solution.py:81
  11.7 0.0 copy-done.1
  11.7 0.8 gather_fusion.1
  12.5 0.0 copy-done.3
  12.5 0.6 dynamic_slice.15
  15.0 13.2 %all-to-all-done = bf16[16,3,5120]{2,1,0:T(4,128)(2,1)S(1)} async-done(((bf16[16,3,5120]{2,1,0:T(4,128)(2,1)}), bf16[16,3,5120]{2,1,0:T(4,128)(2,1)S(1)}, u32[]{:S(2)}, u32[]{:S(2)}) %all-to-all-start) | async-done | bytes 491552 | tf_op jit(solution)/shard_map/all_to_all | solution.py:81
  28.2 0.4 all_to_all.18
  28.6 0.3 convolution_convert_fusion
  29.0 0.2 reshape.153
  29.2 0.2 collective-permute-start
  30.1 0.4 collective-permute-done
  30.5 1.3 %collective-permute-start.1 = (bf16[4,5120]{1,0:T(4,128)(2,1)S(1)}, bf16[4,5120]{1,0:T(4,128)(2,1)S(1)}, u32[]{:S(2)}, u32[]{:S(2)}) collective-permute-start(bf16[4,5120]{1,0:T(4,128)(2,1)S(1)} %broadcast_select_fusion), channel_id=1, source_target_pairs={{0,2},{1,3},{2,0},{3,1},{4,6},{5,7},{6,4},{7,5},{8,10},{9,11},{10,... | collective-permute-start | bytes 122888 | tf_op jit(solution)/shard_map/ppermute | solution.py:18
  31.9 0.0 copy-start.2
  31.9 8.6 %slice_bitcast_fusion.1 = (bf16[12,3,1,128,512]{4,3,1,0,2:T(8,128)(2,1)}, bf16[12,3,1,128,512]{4,3,1,0,2:T(8,128)(2,1)}) fusion(bf16[12,3,2,128,512]{4,3,2,1,0:T(8,128)(2,1)} %bitcast.83), kind=kLoop, calls=%fused_computation.5 | loop fusion | bytes 18874368
  40.4 0.0 copy-done.2
  40.4 0.1 dynamic_slice.14
  40.5 0.0 collective-permute-done.1
  40.6 1.8 %collective-permute-start.2 = (bf16[4,5120]{1,0:T(4,128)(2,1)S(1)}, bf16[4,5120]{1,0:T(4,128)(2,1)S(1)}, u32[]{:S(2)}, u32[]{:S(2)}) collective-permute-start(bf16[4,5120]{1,0:T(4,128)(2,1)S(1)} %broadcast_select_fusion.1), channel_id=1, source_target_pairs={{0,4},{1,5},{2,6},{3,7},{4,0},{5,1},{6,2},{7,3},{8,12},{9,13},{10,... | collective-permute-start | bytes 122888 | tf_op jit(solution)/shard_map/ppermute | solution.py:18
  42.4 0.1 iota_compare_fusion
  42.4 2.2 %collective-permute-done.2 = bf16[4,5120]{1,0:T(4,128)(2,1)S(1)} collective-permute-done((bf16[4,5120]{1,0:T(4,128)(2,1)S(1)}, bf16[4,5120]{1,0:T(4,128)(2,1)S(1)}, u32[]{:S(2)}, u32[]{:S(2)}) %collective-permute-start.2) | collective-permute-done | bytes 40992 | tf_op jit(solution)/shard_map/ppermute | solution.py:18
  44.7 1.8 %collective-permute-start.3 = (bf16[4,5120]{1,0:T(4,128)(2,1)S(1)}, bf16[4,5120]{1,0:T(4,128)(2,1)S(1)}, u32[]{:S(2)}, u32[]{:S(2)}) collective-permute-start(bf16[4,5120]{1,0:T(4,128)(2,1)S(1)} %broadcast_select_fusion.2), channel_id=1, source_target_pairs={{0,8},{1,9},{2,10},{3,11},{4,12},{5,13},{6,14},{7,15},{8,0},{9,1},... | collective-permute-start | bytes 122888 | tf_op jit(solution)/shard_map/ppermute | solution.py:18
  46.4 7.7 %reshape_squeeze.7 = bf16[12,384,4,128]{3,2,1,0:T(4,128)(2,1)} reshape(bf16[12,3,1,128,512]{4,3,1,0,2:T(8,128)(2,1)} %get-tuple-element.6) | data formatting | bytes 9437184 | tf_op jit(solution)/shard_map/reshape;squeeze | solution.py:26
  54.1 7.7 %reshape_squeeze.6 = bf16[12,384,4,128]{3,2,1,0:T(4,128)(2,1)} reshape(bf16[12,3,1,128,512]{4,3,1,0,2:T(8,128)(2,1)} %get-tuple-element.5) | data formatting | bytes 9437184 | tf_op jit(solution)/shard_map/reshape;squeeze | solution.py:25
  61.8 0.0 collective-permute-done.3
  61.9 0.2 slice.24
  62.1 0.4 reshape.154
  62.5 1.9 %fusion.46 = (f32[12,4,4,8]{3,1,2,0:T(4,128)S(1)}, f32[12,4,4,8,4]{3,4,1,2,0:T(4,128)S(1)}) fusion(bf16[12,4,4,8,128]{4,3,2,1,0:T(8,128)(2,1)S(1)} %reshape.154, bf16[12,4,5120]{2,1,0:T(4,128)(2,1)S(1)} %bitcast_dynamic-update-slice_fusion, pred[4,4]{1,0:T(4,128)(4,1)S(1)} %iota_compare_fusion.7), kind=kOutput, calls=%fused_computation.89 | convolution fusion | flops 1589760 | bytes 473600 | tf_op jit(solution)/shard_map/rtghd,rugd->rtghu/dot_general | solution.py:36
  64.3 0.0 slice-start
  64.4 0.0 slice-start.1
  64.4 4.3 %bitcast_reduce_fusion = (f32[12,4,4,8]{3,1,2,0:T(4,128)S(1)}, f32[12,4,4,8,384]{4,3,2,1,0:T(8,128)S(1)}) fusion(pred[12,384]{1,0:T(8,128)(4,1)S(1)} %iota_compare_fusion, bf16[12,384,4,128,1]{3,2,1,0,4:T(4,128)(2,1)} %bitcast.82, bf16[12,4,4,8,128]{4,3,2,1,0:T(8,128)(2,1)S(1)} %reshape.154), kind=kOutput, calls=%fused_computation.13 | convolution fusion | flops 152762880 | bytes 7481856 | tf_op jit(solution)/shard_map/rtghd,rlgd->rtghl/dot_general | solution.py:32
  68.8 0.9 fusion.6
  69.7 0.0 slice-done
  69.7 0.0 slice-done.1
  69.7 1.2 %fusion.8 = f32[12,4,4,8,128]{4,3,1,2,0:T(8,128)S(1)} fusion(bf16[12,384,4,128,1]{3,2,1,0,4:T(4,128)(2,1)S(1)} %bitcast.86, f32[12,4,4,8,384]{4,3,2,1,0:T(8,128)S(1)} %get-tuple-element.8, f32[12,4,4,8]{3,1,2,0:T(4,128)S(1)} %max.7, pred[12,384]{1,0:T(8,128)(4,1)S(1)} %iota_compare_fusion), kind=kOutput, calls=%fused_computation.19 | convolution fusion | flops 153944064 | bytes 7875072 | tf_op jit(solution)/shard_map/rtghl,rlgd->rtghd/dot_general | solution.py:50
  70.9 0.4 fusion.25
  71.4 0.5 fusion.13
  71.9 0.1 copy.16
  72.0 0.1 convert_element_type.31
  72.1 0.1 collective-permute-start.4
  72.2 1.2 %collective-permute-done.4 = bf16[4,4096]{1,0:T(4,128)(2,1)S(1)} collective-permute-done((bf16[4,4096]{1,0:T(4,128)(2,1)S(1)}, bf16[4,4096]{1,0:T(4,128)(2,1)S(1)}, u32[]{:S(2)}, u32[]{:S(2)}) %collective-permute-start.4) | collective-permute-done | bytes 32800 | tf_op jit(solution)/shard_map/ppermute | solution.py:18
  73.4 2.1 %collective-permute-start.5 = (bf16[4,4096]{1,0:T(4,128)(2,1)S(1)}, bf16[4,4096]{1,0:T(4,128)(2,1)S(1)}, u32[]{:S(2)}, u32[]{:S(2)}) collective-permute-start(bf16[4,4096]{1,0:T(4,128)(2,1)S(1)} %broadcast_select_fusion.3), channel_id=1, source_target_pairs={{0,2},{1,3},{2,0},{3,1},{4,6},{5,7},{6,4},{7,5},{8,10},{9,11},{10,... | collective-permute-start | bytes 98312 | tf_op jit(solution)/shard_map/ppermute | solution.py:18
  75.5 1.9 %collective-permute-done.5 = bf16[4,4096]{1,0:T(4,128)(2,1)S(1)} collective-permute-done((bf16[4,4096]{1,0:T(4,128)(2,1)S(1)}, bf16[4,4096]{1,0:T(4,128)(2,1)S(1)}, u32[]{:S(2)}, u32[]{:S(2)}) %collective-permute-start.5) | collective-permute-done | bytes 32800 | tf_op jit(solution)/shard_map/ppermute | solution.py:18
  77.4 1.6 %collective-permute-start.6 = (bf16[4,4096]{1,0:T(4,128)(2,1)S(1)}, bf16[4,4096]{1,0:T(4,128)(2,1)S(1)}, u32[]{:S(2)}, u32[]{:S(2)}) collective-permute-start(bf16[4,4096]{1,0:T(4,128)(2,1)S(1)} %broadcast_select_fusion.4), channel_id=1, source_target_pairs={{0,4},{1,5},{2,6},{3,7},{4,0},{5,1},{6,2},{7,3},{8,12},{9,13},{10,... | collective-permute-start | bytes 98312 | tf_op jit(solution)/shard_map/ppermute | solution.py:18
  79.0 2.4 %collective-permute-done.6 = bf16[4,4096]{1,0:T(4,128)(2,1)S(1)} collective-permute-done((bf16[4,4096]{1,0:T(4,128)(2,1)S(1)}, bf16[4,4096]{1,0:T(4,128)(2,1)S(1)}, u32[]{:S(2)}, u32[]{:S(2)}) %collective-permute-start.6) | collective-permute-done | bytes 32800 | tf_op jit(solution)/shard_map/ppermute | solution.py:18
  81.4 1.3 %collective-permute-start.7 = (bf16[4,4096]{1,0:T(4,128)(2,1)S(1)}, bf16[4,4096]{1,0:T(4,128)(2,1)S(1)}, u32[]{:S(2)}, u32[]{:S(2)}) collective-permute-start(bf16[4,4096]{1,0:T(4,128)(2,1)S(1)} %broadcast_select_fusion.5), channel_id=1, source_target_pairs={{0,8},{1,9},{2,10},{3,11},{4,12},{5,13},{6,14},{7,15},{8,0},{9,1},... | collective-permute-start | bytes 98312 | tf_op jit(solution)/shard_map/ppermute | solution.py:18
  82.7 3.6 %collective-permute-done.7 = bf16[4,4096]{1,0:T(4,128)(2,1)S(1)} collective-permute-done((bf16[4,4096]{1,0:T(4,128)(2,1)S(1)}, bf16[4,4096]{1,0:T(4,128)(2,1)S(1)}, u32[]{:S(2)}, u32[]{:S(2)}) %collective-permute-start.7) | collective-permute-done | bytes 32800 | tf_op jit(solution)/shard_map/ppermute | solution.py:18
  86.3 0.1 reshape.158
  86.4 0.4 convolution_convert_fusion.3
  86.8 0.2 all_to_all.19
  87.0 18.3 %all_to_all.24 = bf16[16,3,4096]{2,1,0:T(4,128)(2,1)S(1)} all-to-all(bf16[16,3,4096]{2,1,0:T(4,128)(2,1)S(1)} %all_to_all.19), channel_id=1, replica_groups=mesh['groups'=2,'req'=16] {'req'}, dimensions={0} | all-to-all | bytes 786432 | tf_op jit(solution)/shard_map/all_to_all | solution.py:110
  105.4 0.3 all_to_all.21
  105.7 1.1 convolution_convert_fusion.2
  (18 shorter events, 0.4 us)
Async XLA Ops:
  0.0 2.9 %copy-start = (bf16[48,5120]{1,0:T(8,128)(2,1)S(1)}, bf16[48,5120]{1,0:T(8,128)(2,1)}, u32[]{:S(2)}) copy-start(bf16[48,5120]{1,0:T(8,128)(2,1)} %param.8) | copy-start | bytes 1474564
  0.0 11.7 %copy-start.1 = (s32[16]{0:T(128)S(1)}, s32[16]{0:T(128)}, u32[]{:S(2)}) copy-start(s32[16]{0:T(128)} %param.10) | copy-start | bytes 196
  0.0 12.5 %copy-start.3 = (s32[16]{0:T(128)S(1)}, s32[16]{0:T(128)}, u32[]{:S(2)}) copy-start(s32[16]{0:T(128)} %param.13) | copy-start | bytes 196
  4.3 24.0 %all-to-all-start = ((bf16[16,3,5120]{2,1,0:T(4,128)(2,1)}), bf16[16,3,5120]{2,1,0:T(4,128)(2,1)S(1)}, u32[]{:S(2)}, u32[]{:S(2)}) async-start(bf16[16,3,5120]{2,1,0:T(4,128)(2,1)} %all_to_all.16), calls=%async_computation | async-start | bytes 1310720 | tf_op jit(solution)/shard_map/all_to_all | solution.py:81
  29.2 1.3 %collective-permute-start = (bf16[4,5120]{1,0:T(4,128)(2,1)S(1)}, bf16[4,5120]{1,0:T(4,128)(2,1)S(1)}, u32[]{:S(2)}, u32[]{:S(2)}) collective-permute-start(bf16[4,5120]{1,0:T(4,128)(2,1)S(1)} %dynamic-slice_bitcast_fusion), channel_id=1, source_target_pairs={{0,1},{1,0},{2,3},{3,2},{4,5},{5,4},{6,7},{7,6},{8,9},{9,8},{10,11... | collective-permute-start | bytes 122888 | tf_op jit(solution)/shard_map/ppermute | solution.py:18
  30.5 10.0 %collective-permute-start.1 = (bf16[4,5120]{1,0:T(4,128)(2,1)S(1)}, bf16[4,5120]{1,0:T(4,128)(2,1)S(1)}, u32[]{:S(2)}, u32[]{:S(2)}) collective-permute-start(bf16[4,5120]{1,0:T(4,128)(2,1)S(1)} %broadcast_select_fusion), channel_id=1, source_target_pairs={{0,2},{1,3},{2,0},{3,1},{4,6},{5,7},{6,4},{7,5},{8,10},{9,11},{10,... | collective-permute-start | bytes 122888 | tf_op jit(solution)/shard_map/ppermute | solution.py:18
  31.9 8.6 %copy-start.2 = (s32[192]{0:T(256)S(1)}, s32[192]{0:T(256)}, u32[]{:S(2)}) copy-start(s32[192]{0:T(256)} %param.9) | copy-start | bytes 2308
  40.6 4.1 %collective-permute-start.2 = (bf16[4,5120]{1,0:T(4,128)(2,1)S(1)}, bf16[4,5120]{1,0:T(4,128)(2,1)S(1)}, u32[]{:S(2)}, u32[]{:S(2)}) collective-permute-start(bf16[4,5120]{1,0:T(4,128)(2,1)S(1)} %broadcast_select_fusion.1), channel_id=1, source_target_pairs={{0,4},{1,5},{2,6},{3,7},{4,0},{5,1},{6,2},{7,3},{8,12},{9,13},{10,... | collective-permute-start | bytes 122888 | tf_op jit(solution)/shard_map/ppermute | solution.py:18
  44.7 17.2 %collective-permute-start.3 = (bf16[4,5120]{1,0:T(4,128)(2,1)S(1)}, bf16[4,5120]{1,0:T(4,128)(2,1)S(1)}, u32[]{:S(2)}, u32[]{:S(2)}) collective-permute-start(bf16[4,5120]{1,0:T(4,128)(2,1)S(1)} %broadcast_select_fusion.2), channel_id=1, source_target_pairs={{0,8},{1,9},{2,10},{3,11},{4,12},{5,13},{6,14},{7,15},{8,0},{9,1},... | collective-permute-start | bytes 122888 | tf_op jit(solution)/shard_map/ppermute | solution.py:18
  64.3 5.3 %slice-start = ((s8[4718592]{0:T(1024)(128)(4,1)}), s8[4194304]{0:T(1024)(128)(4,1)S(1)}, s32[]{:S(2)}) async-start(s8[4718592]{0:T(1024)(128)(4,1)} %bitcast.84), calls=%async_computation.2 | async-start | bytes 8388608
  64.4 5.3 %slice-start.1 = ((s8[4718592]{0:T(1024)(128)(4,1)}), s8[524288]{0:T(1024)(128)(4,1)S(1)}, s32[]{:S(2)}) async-start(s8[4718592]{0:T(1024)(128)(4,1)} %bitcast.84), calls=%async_computation.3 | async-start | bytes 1048576
  72.1 1.3 %collective-permute-start.4 = (bf16[4,4096]{1,0:T(4,128)(2,1)S(1)}, bf16[4,4096]{1,0:T(4,128)(2,1)S(1)}, u32[]{:S(2)}, u32[]{:S(2)}) collective-permute-start(bf16[4,4096]{1,0:T(4,128)(2,1)S(1)} %dynamic-slice_bitcast_fusion.1), channel_id=1, source_target_pairs={{0,1},{1,0},{2,3},{3,2},{4,5},{5,4},{6,7},{7,6},{8,9},{9,8},{10,11... | collective-permute-start | bytes 98312 | tf_op jit(solution)/shard_map/ppermute | solution.py:18
  73.4 4.0 %collective-permute-start.5 = (bf16[4,4096]{1,0:T(4,128)(2,1)S(1)}, bf16[4,4096]{1,0:T(4,128)(2,1)S(1)}, u32[]{:S(2)}, u32[]{:S(2)}) collective-permute-start(bf16[4,4096]{1,0:T(4,128)(2,1)S(1)} %broadcast_select_fusion.3), channel_id=1, source_target_pairs={{0,2},{1,3},{2,0},{3,1},{4,6},{5,7},{6,4},{7,5},{8,10},{9,11},{10,... | collective-permute-start | bytes 98312 | tf_op jit(solution)/shard_map/ppermute | solution.py:18
  77.4 4.0 %collective-permute-start.6 = (bf16[4,4096]{1,0:T(4,128)(2,1)S(1)}, bf16[4,4096]{1,0:T(4,128)(2,1)S(1)}, u32[]{:S(2)}, u32[]{:S(2)}) collective-permute-start(bf16[4,4096]{1,0:T(4,128)(2,1)S(1)} %broadcast_select_fusion.4), channel_id=1, source_target_pairs={{0,4},{1,5},{2,6},{3,7},{4,0},{5,1},{6,2},{7,3},{8,12},{9,13},{10,... | collective-permute-start | bytes 98312 | tf_op jit(solution)/shard_map/ppermute | solution.py:18
  81.4 4.9 %collective-permute-start.7 = (bf16[4,4096]{1,0:T(4,128)(2,1)S(1)}, bf16[4,4096]{1,0:T(4,128)(2,1)S(1)}, u32[]{:S(2)}, u32[]{:S(2)}) collective-permute-start(bf16[4,4096]{1,0:T(4,128)(2,1)S(1)} %broadcast_select_fusion.5), channel_id=1, source_target_pairs={{0,8},{1,9},{2,10},{3,11},{4,12},{5,13},{6,14},{7,15},{8,0},{9,1},... | collective-permute-start | bytes 98312 | tf_op jit(solution)/shard_map/ppermute | solution.py:18
where the time goes:
time: 107 us
  local copies, waits for them, and re-layouts  30.1 us (28%)
  waiting for transfers between devices  24.9 us (23%)
  blocking collectives  18.3 us (17%)
  starting transfers between devices  17.6 us (16%)
  matrix products  9.96 us (9%)
  other arithmetic  3.14 us (3%)
  between operations  2.85 us (3%)
    all_to_all x1, blocking collectives, on_device(): lax.all_to_all(backward, 'req', split_axis=0, concat_axis=0, tiled=True)  18.3 us
    all_to_all x1, waiting for transfers between devices, on_device(): lax.all_to_all(outgoing, 'req', split_axis=0, concat_axis=0, tiled=True)  13.2 us
    ppermute x8, waiting for transfers between devices, from_partner(): lax.ppermute(value, axis, [(i, i ^ 1 << apart) for i in range(lax.axis_si...  11.6 us
    ppermute x8, starting transfers between devices, from_partner(): lax.ppermute(value, axis, [(i, i ^ 1 << apart) for i in range(lax.axis_si...  10.2 us
    unnamed x13, local copies, waits for them, and re-layouts  8.61 us
    another operation x1, local copies, waits for them, and re-layouts, attend_slots(): cache_vals = page_pool[:, :, 1].reshape(slots, span, KVH, HD)  7.73 us
    another operation x1, local copies, waits for them, and re-layouts, attend_slots(): cache_keys = page_pool[:, :, 0].reshape(slots, span, KVH, HD)  7.7 us
    all_to_all x1, starting transfers between devices, on_device(): lax.all_to_all(outgoing, 'req', split_axis=0, concat_axis=0, tiled=True)  7.4 us
  transfers between devices with their start and end apart: 9, of which 7 were waited for; matrix products, arithmetic and copies ran while one was open for 24% of the time, Pallas kernels for 0%

commit v1 on v0

v1 whole, which is shorter than its diff:
```python
import functools

import jax
import jax.numpy as jnp
from jax import lax
from jax.experimental import pallas as pl
from jax.experimental.pallas import tpu as pltpu
from jax.sharding import PartitionSpec as P

HD = 128
DRAFT = 4
PAGE = 128
R_DEV = 12
PPR = 3
QW = 4096
KVW = 512
KVH = KVW // HD
GRP = QW // KVW
LANES = 128
WIDE = QW // GRP + LANES
SPAN = R_DEV * GRP * DRAFT
SLOT = GRP * DRAFT
BF = jnp.bfloat16
F32 = jnp.float32
I32 = jnp.int32
VMEM = pl.BlockSpec(memory_space=pltpu.VMEM)
SMEM = pl.BlockSpec(memory_space=pltpu.SMEM)


def iota(shape, dim):
    return lax.broadcasted_iota(I32, shape, dim)


def onehot(mask):
    return jnp.where(mask, jnp.float32(1), jnp.float32(0)).astype(BF)


def exact_dot(a, b):
    return jnp.dot(a, b, preferred_element_type=F32)


def stacked(value, cap):
    width = value.shape[1] // cap
    return jnp.concatenate([value[:, r * width : (r + 1) * width] for r in range(cap)], axis=0)


def wrapped(value, count):
    value = jnp.where(value < 0, value + count, value)
    return jnp.where(value >= count, value - count, value)


def peers_of(k, offs_ref, cap, sign, me, count):
    off = jnp.full(k.shape, offs_ref[0], I32)
    first = jnp.zeros(k.shape, I32)
    for i in range(1, offs_ref.shape[0]):
        off = jnp.where(k >= i * cap, offs_ref[i], off)
        first = jnp.where(k >= i * cap, i * cap, first)
    return wrapped(me + sign * off, count), k - first


def pack_kernel(count, cap, order_ref, offs_ref, rows_ref, out_ref, stack_ref):
    rows = rows_ref.shape[0]
    for h in range(GRP):
        for g in range(KVH):
            c = (g * GRP + h) * HD
            stack_ref[h * rows : (h + 1) * rows, g * HD : (g + 1) * HD] = rows_ref[:, c : c + HD]
        c = QW + h * HD
        stack_ref[h * rows : (h + 1) * rows, KVH * HD :] = rows_ref[:, c : c + HD]
    me = lax.axis_index("req")
    k = order_ref[...]
    peer, place = peers_of(k, offs_ref, cap, -1, me, count)
    wide = GRP * rows
    lane = iota((rows, wide), 1)
    tile = functools.reduce(
        jnp.logical_or, [lane == iota((rows, wide), 0) + h * rows for h in range(GRP)]
    )
    tile = onehot(tile)
    peer = exact_dot(jnp.broadcast_to(peer.astype(F32), (8, rows)).astype(BF), tile)[:1]
    place = exact_dot(jnp.broadcast_to(place.astype(F32), (8, rows)).astype(BF), tile)[:1]
    lane = iota((1, wide), 1)
    part = sum([(lane >= h * rows).astype(I32) for h in range(1, GRP)])
    spot = peer.astype(I32) * GRP + part
    at = iota((count * GRP, wide), 0)
    for r in range(cap):
        here = jnp.where(place.astype(I32) == r, spot, -1)
        out_ref[:, r * WIDE : (r + 1) * WIDE] = exact_dot(onehot(at == here), stack_ref[...]).astype(BF)


def visitor_kernel(count, cap, offs_ref, moved_ref, in_ref, out_ref):
    me = lax.axis_index("req")
    slot = moved_ref[me]
    wide = cap * count * GRP
    row = iota((SLOT, wide), 0)
    spot = jnp.zeros((SLOT, wide), I32)
    for t in range(DRAFT):
        k = slot * DRAFT + t
        c = k // cap
        peer = wrapped(me + offs_ref[c], count)
        spot = jnp.where((row & (DRAFT - 1)) == t, (k - c * cap) * (count * GRP) + peer * GRP, spot)
    pick = onehot(iota((SLOT, wide), 1) == spot + (row >> 2))
    out_ref[...] = exact_dot(pick, stacked(in_ref[...], cap)).astype(BF)


def attend_kernel(
    count, cap, offs_ref, moved_ref, lengths_ref, in_ref, visitor_ref, kv_ref, out_ref, answer_ref, rows_ref, sums_ref
):
    me = lax.axis_index("req")
    row = iota((SPAN, LANES), 0)
    k = (row >> 5) * DRAFT + (row & (DRAFT - 1))
    peer, place = peers_of(k, offs_ref, cap, 1, me, count)
    spot = place * (count * GRP) + peer * GRP + ((row >> 2) & (GRP - 1))
    lane = iota((SPAN, LANES), 1)
    blocks = cap * count * GRP // LANES
    pick = jnp.concatenate([onehot(spot - b * LANES == lane) for b in range(blocks)], axis=1)
    rows_ref[...] = exact_dot(pick, stacked(in_ref[...], cap)).astype(BF)
    moved = pl.multiple_of(moved_ref[me] * SLOT, SLOT)
    rows_ref[pl.ds(moved, SLOT), :] = visitor_ref[...]
    row = iota((SPAN, SPAN), 0)
    lane = iota((SPAN, SPAN), 1)
    fresh = R_DEV * DRAFT
    turned = functools.reduce(
        jnp.logical_or,
        [
            (row - s * fresh == (lane >> 5) * DRAFT + (lane & (DRAFT - 1))) & (((lane >> 2) & (GRP - 1)) == s)
            for s in range(GRP)
        ],
    )
    fresh_kv = exact_dot(onehot(turned), rows_ref[:, KVH * HD :]).astype(BF)
    factor = 1.0 / jnp.sqrt(jnp.float32(HD))
    row = iota((SPAN, fresh), 0)
    lane = iota((SPAN, fresh), 1)
    seen = ((row >> 5) == (lane >> 2)) & ((lane & (DRAFT - 1)) <= (row & (DRAFT - 1)))
    position = iota((SLOT, PPR * PAGE), 1)
    contract = (((1,), (1,)), ((), ()))
    for g in range(KVH):
        cols = slice(g * HD, (g + 1) * HD)
        new_keys = fresh_kv[g * fresh : (g + 1) * fresh]
        new_vals = fresh_kv[(KVH + g) * fresh : (KVH + g + 1) * fresh]
        new_score = lax.dot_general(rows_ref[:, cols], new_keys, contract, preferred_element_type=F32) * factor
        new_score = jnp.where(seen, new_score, jnp.float32(-1e30))
        new_peak = jnp.max(new_score, axis=1, keepdims=True)
        for s in range(R_DEV):
            mine = slice(s * SLOT, (s + 1) * SLOT)
            length = lengths_ref[me * R_DEV + s]
            keys = jnp.concatenate([kv_ref[s * PPR + p, 0, :, cols] for p in range(PPR)], axis=0)
            vals = jnp.concatenate([kv_ref[s * PPR + p, 1, :, cols] for p in range(PPR)], axis=0)
            score = lax.dot_general(rows_ref[mine, cols], keys, contract, preferred_element_type=F32) * factor
            score = jnp.where(position < length, score, jnp.float32(-1e30))
            peak = jnp.maximum(jnp.max(score, axis=1, keepdims=True), new_peak[mine])
            weight = jnp.exp(score - peak)
            new_weight = jnp.exp(new_score[mine] - peak)
            total = jnp.sum(weight, axis=1, keepdims=True) + jnp.sum(new_weight, axis=1, keepdims=True)
            summed = exact_dot(weight.astype(BF), vals) + exact_dot(new_weight.astype(BF), new_vals)
            out_ref[mine, cols] = (summed / total).astype(BF)
    answer_ref[...] = out_ref[pl.ds(moved, SLOT), :]


def reply_kernel(count, cap, offs_ref, moved_ref, rows_in_ref, answer_ref, out_ref, rows_ref):
    me = lax.axis_index("req")
    rows_ref[...] = rows_in_ref[...]
    moved = pl.multiple_of(moved_ref[me] * SLOT, SLOT)
    rows_ref[pl.ds(moved, SLOT), :] = answer_ref[...]
    lane = iota((1, SPAN), 1)
    k = (lane >> 5) * DRAFT + (lane & (DRAFT - 1))
    peer, place = peers_of(k, offs_ref, cap, 1, me, count)
    spot = peer * GRP + ((lane >> 2) & (GRP - 1))
    at = iota((count * GRP, SPAN), 0)
    for r in range(cap):
        here = jnp.where(place == r, spot, -1)
        out_ref[:, r * KVW : (r + 1) * KVW] = exact_dot(onehot(at == here), rows_ref[...]).astype(BF)


def finish_kernel(count, cap, order_ref, offs_ref, in_ref, out_ref):
    rows = out_ref.shape[0]
    me = lax.axis_index("req")
    peer, place = peers_of(order_ref[...], offs_ref, cap, -1, me, count)
    spot = place * (count * GRP) + peer * GRP
    same = iota((rows, rows), 0) == iota((rows, rows), 1)
    spot = jnp.sum(jnp.where(same, spot, 0).astype(F32), axis=1, keepdims=True).astype(I32)
    wide = cap * count * GRP
    lane = iota((rows, wide), 1)
    pick = jnp.concatenate([onehot(lane == spot + h) for h in range(GRP)], axis=0)
    result = exact_dot(pick, stacked(in_ref[...], cap)).astype(BF)
    for h in range(GRP):
        for g in range(KVH):
            c = (g * GRP + h) * HD
            out_ref[:, c : c + HD] = result[h * rows : (h + 1) * rows, g * HD : (g + 1) * HD]


def hop(value, mask, count):
    step = 1
    while step < count:
        choices = min(16, count // step)
        digit = jnp.bitwise_and(mask // step, choices - 1)
        only = choices == count
        branches = [
            functools.partial(
                lambda by, v: lax.ppermute(v, "req", [(i, i ^ by) for i in range(count)]), d * step
            )
            for d in range(1, choices)
        ]
        if only:
            value = lax.switch(digit - 1, branches, value)
        else:
            value = lax.switch(digit, [lambda v: v] + branches, value)
        step *= choices
    return value


def on_device(kv_cache, draft_rows, cache_lengths, row_offsets, draft_order, pair_mask, moved_slots):
    count = lax.axis_size("req")
    rows = draft_rows.shape[0]
    cap = max(1, rows // count)
    order = draft_order.reshape(1, rows)
    mask = pair_mask[0]

    def call(kernel, specs, outs, scratch=()):
        return pl.pallas_call(
            functools.partial(kernel, count, cap),
            in_specs=specs,
            out_specs=[VMEM] * len(outs) if len(outs) > 1 else VMEM,
            out_shape=[jax.ShapeDtypeStruct(o, BF) for o in outs] if len(outs) > 1 else jax.ShapeDtypeStruct(outs[0], BF),
            scratch_shapes=[pltpu.VMEM(s, BF) for s in scratch],
        )

    outgoing = call(
        pack_kernel, [VMEM, SMEM, VMEM], [(count * GRP, cap * WIDE)], [(GRP * rows, WIDE)]
    )(order, row_offsets, draft_rows)
    incoming = lax.all_to_all(outgoing, "req", split_axis=0, concat_axis=0, tiled=True)
    visitor = call(visitor_kernel, [SMEM, SMEM, VMEM], [(SLOT, WIDE)])(row_offsets, moved_slots, incoming)
    visitor = hop(visitor, mask, count)
    results, answer = call(
        attend_kernel, [SMEM, SMEM, SMEM, VMEM, VMEM, VMEM], [(SPAN, KVW), (SLOT, KVW)], [(SPAN, WIDE), (8, 128)]
    )(row_offsets, moved_slots, cache_lengths, incoming, visitor, kv_cache)
    answer = hop(answer, mask, count)
    backward = call(reply_kernel, [SMEM, SMEM, VMEM, VMEM], [(count * GRP, cap * KVW)], [(SPAN, KVW)])(
        row_offsets, moved_slots, results, answer
    )
    returned = lax.all_to_all(backward, "req", split_axis=0, concat_axis=0, tiled=True)
    return call(finish_kernel, [VMEM, SMEM, VMEM], [(rows, QW)])(order, row_offsets, returned)


def solution(mesh):
    in_specs = (
        P(("groups", "req"), None, None, None),
        P(("groups", "req"), None),
        P("groups"),
        P("groups"),
        P(("groups", "req")),
        P("groups"),
        P("groups"),
    )
    out_specs = P(("groups", "req"), None)
    return jax.shard_map(
        on_device, mesh=mesh, in_specs=in_specs, out_specs=out_specs, check_vma=False
    )
```

time: 107 us -> 77.2 us (0.72)
  local copies, waits for them, and re-layouts: 30.1 us -> 0.77 us
  Pallas kernels: 0 us -> 28 us
  matrix products: 9.96 us -> 0 us
  starting transfers between devices: 17.6 us -> 9.65 us
  waiting for transfers between devices: 24.9 us -> 21.2 us
  other arithmetic: 3.14 us -> 0 us
  between operations: 2.85 us -> 0.67 us
  blocking collectives: 18.3 us -> 16.4 us
    pallas_call x0 -> x5, Pallas kernels: none -> 28 us  [the longest x1 19.9 us: on_device(): call(attend_kernel, [SMEM, SMEM, SMEM, VMEM, VMEM, VMEM], [(SPAN, KVW), (...]
    another operation x2 -> x0, local copies, waits for them, and re-layouts: 15.4 us -> none  [the longest x1 7.73 us: attend_slots(): cache_vals = page_pool[:, :, 1].reshape(slots, span, KVH, HD)]
    dot_general x8 -> x0, matrix products: 9.96 us -> none  [the longest x1 4.34 us: attend_slots(): jnp.einsum('rtghd,rlgd->rtghl', queries, cache_keys, preferred_element_ty...]
    ppermute x8 -> x2, starting transfers between devices: 10.2 us -> 2.27 us  [hop(): lax.ppermute(v, 'req', [(i, i ^ by) for i in range(count)])]
    unnamed x13 -> x2, local copies, waits for them, and re-layouts: 8.61 us -> 0.77 us
    ppermute x8 -> x2, waiting for transfers between devices: 11.6 us -> 8.15 us  [hop(): lax.ppermute(v, 'req', [(i, i ^ by) for i in range(count)])]
    gather x2 -> x0, local copies, waits for them, and re-layouts: 2.21 us -> none  [the longest x1 1.43 us: on_device(): targets = (own_index - row_offsets[draft_order // per_peer]) % count]
    all_to_all x4 -> x0, local copies, waits for them, and re-layouts: 2.1 us -> none  [the longest x2 1.54 us: on_device(): lax.all_to_all(outgoing, 'req', split_axis=0, concat_axis=0, tiled=True)]
  transfers between devices with their start and end apart: 9 -> 3, of which waited for: 7 -> 3; matrix products, arithmetic and copies ran while one was open for 24% -> 0% of each run, Pallas kernels for 0% -> 0%
where the time goes in v1:
time: 77.2 us; the launch traced here: 76.8 us
  Pallas kernels  28 us (36%)
  waiting for transfers between devices  21.2 us (27%)
  blocking collectives  16.4 us (21%)
  starting transfers between devices  9.65 us (12%)
    pallas_call x1, Pallas kernels, on_device(): call(attend_kernel, [SMEM, SMEM, SMEM, VMEM, VMEM, VMEM], [(SPAN, KVW), (...  19.9 us
    all_to_all x1, blocking collectives, on_device(): lax.all_to_all(backward, 'req', split_axis=0, concat_axis=0, tiled=True)  16.4 us
    all_to_all x1, waiting for transfers between devices, on_device(): lax.all_to_all(outgoing, 'req', split_axis=0, concat_axis=0, tiled=True)  13.1 us
    ppermute x2, waiting for transfers between devices, hop(): lax.ppermute(v, 'req', [(i, i ^ by) for i in range(count)])  8.15 us
    all_to_all x1, starting transfers between devices, on_device(): lax.all_to_all(outgoing, 'req', split_axis=0, concat_axis=0, tiled=True)  7.38 us
    pallas_call x1, Pallas kernels, on_device(): call(pack_kernel, [VMEM, SMEM, VMEM], [(count * GRP, cap * WIDE)], [(GRP...  2.44 us
    ppermute x2, starting transfers between devices, hop(): lax.ppermute(v, 'req', [(i, i ^ by) for i in range(count)])  2.27 us
    pallas_call x1, Pallas kernels, on_device(): call(finish_kernel, [VMEM, SMEM, VMEM], [(rows, QW)])  2.26 us
  transfers between devices with their start and end apart: 3, of which 3 were waited for; matrix products, arithmetic and copies ran while one was open for 0% of the time, Pallas kernels for 0%

profile of v1, /device:TPU:0, one launch (start us, length us, event | category | flops | bytes accessed | tf_op | source)
XLA Modules:
  0.0 76.8 jit_solution(17183345119201366718)
XLA Ops:
  0.0 2.4 %shard_map.73 = bf16[128,1920]{1,0:T(8,128)(2,1)} custom-call(s32[1,48]{1,0:T(1,128)} %bitcast.11, s32[16]{0:T(128)} %offs_ref.9, bf16[48,5120]{1,0:T(8,128)(2,1)} %rows_ref.1), custom_call_target="tpu_custom_call" | custom-call | tf_op jit(solution)/shard_map/pallas_call | solution.py:226
  2.4 7.4 %all-to-all-start = ((bf16[16,8,1920]{2,1,0:T(8,128)(2,1)}), bf16[16,8,1920]{2,1,0:T(8,128)(2,1)S(1)}, u32[]{:S(2)}, u32[]{:S(2)}) async-start(bf16[16,8,1920]{2,1,0:T(8,128)(2,1)} %bitcast.8), calls=%async_computation | async-start | bytes 983040 | tf_op jit(solution)/shard_map/all_to_all | solution.py:229
  10.5 13.1 %all-to-all-done = bf16[16,8,1920]{2,1,0:T(8,128)(2,1)S(1)} async-done(((bf16[16,8,1920]{2,1,0:T(8,128)(2,1)}), bf16[16,8,1920]{2,1,0:T(8,128)(2,1)S(1)}, u32[]{:S(2)}, u32[]{:S(2)}) %all-to-all-start) | async-done | bytes 491552 | tf_op jit(solution)/shard_map/all_to_all | solution.py:229
  23.6 0.0 copy-start
  23.6 0.8 %copy-done = bf16[16,8,1920]{2,1,0:T(8,128)(2,1)} copy-done((bf16[16,8,1920]{2,1,0:T(8,128)(2,1)}, bf16[16,8,1920]{2,1,0:T(8,128)(2,1)S(1)}, u32[]{:S(2)}) %copy-start) | copy-done | bytes 491544
  24.4 1.2 %shard_map.74 = bf16[32,640]{1,0:T(8,128)(2,1)S(1)} custom-call(s32[16]{0:T(128)} %offs_ref.9, s32[16]{0:T(128)} %moved_ref.5, bf16[128,1920]{1,0:T(8,128)(2,1)} %bitcast.6), custom_call_target="tpu_custom_call" | custom-call | tf_op jit(solution)/shard_map/pallas_call | solution.py:230
  25.6 5.1 %conditional.2 = (bf16[32,640]{1,0:T(8,128)(2,1)}) conditional(s32[]{:T(128)} %bitcast.3, bf16[32,640]{1,0:T(8,128)(2,1)S(1)} %shard_map.74, bf16[32,640]{1,0:T(8,128)(2,1)S(1)} %shard_map.74, bf16[32,640]{1,0:T(8,128)(2,1)S(1)} %shard_map.74, bf16[32,640]{1,0:T(8,128)(2,1)S(1)} %shard_map.74, ...), branch_computations={%region_0.1_spmd, %region_1.2_spmd, %region_2.3_spmd, %region_3.4_... | conditional | bytes 163888 | solution.py:203
  25.7 1.3 %collective-permute-start.8 = (bf16[32,640]{1,0:T(8,128)(2,1)S(1)}, bf16[32,640]{1,0:T(8,128)(2,1)}, u32[]{:S(2)}, u32[]{:S(2)}) collective-permute-start(bf16[32,640]{1,0:T(8,128)(2,1)S(1)} %param.8), channel_id=1, source_target_pairs={{0,9},{1,8},{2,11},{3,10},{4,13},{5,12},{6,15},{7,14},{8,1},{9,0},... | collective-permute-start | bytes 122888 | tf_op jit(solution)/shard_map/cond/branch_8_fun/ppermute | solution.py:198
  27.0 3.8 %collective-permute-done.8 = bf16[32,640]{1,0:T(8,128)(2,1)} collective-permute-done((bf16[32,640]{1,0:T(8,128)(2,1)S(1)}, bf16[32,640]{1,0:T(8,128)(2,1)}, u32[]{:S(2)}, u32[]{:S(2)}) %collective-permute-start.8) | collective-permute-done | bytes 40992 | tf_op jit(solution)/shard_map/cond/branch_8_fun/ppermute | solution.py:198
  30.7 19.9 %shard_map.75 = (bf16[384,512]{1,0:T(8,128)(2,1)}, bf16[32,512]{1,0:T(8,128)(2,1)S(1)}) custom-call(s32[16]{0:T(128)} %offs_ref.9, s32[16]{0:T(128)} %moved_ref.5, s32[192]{0:T(256)} %lengths_ref.1, bf16[128,1920]{1,0:T(8,128)(2,1)} %bitcast.7, bf16[32,640]{1,0:T(8,128)(2,1)} %get-tuple-element.71.visitor_ref, bf16[36,2,128,512]{3,2,1,0:T(8,128)(2,1)} %kv_ref.1), custom_call_target="tpu_custom_call" | custom-call | tf_op jit(solution)/shard_map/pallas_call | solution.py:232
  50.6 5.3 %conditional.3 = (bf16[32,512]{1,0:T(8,128)(2,1)}) conditional(s32[]{:T(128)} %bitcast.3, bf16[32,512]{1,0:T(8,128)(2,1)S(1)} %get-tuple-element.70, bf16[32,512]{1,0:T(8,128)(2,1)S(1)} %get-tuple-element.70, bf16[32,512]{1,0:T(8,128)(2,1)S(1)} %get-tuple-element.70, ...), branch_computations={%region_15.16_spmd, %region_16.17_spmd, %region_17.18_spmd, %regio... | conditional | bytes 131120 | solution.py:203
  50.6 1.0 %collective-permute-start.23 = (bf16[32,512]{1,0:T(8,128)(2,1)S(1)}, bf16[32,512]{1,0:T(8,128)(2,1)}, u32[]{:S(2)}, u32[]{:S(2)}) collective-permute-start(bf16[32,512]{1,0:T(8,128)(2,1)S(1)} %param.23), channel_id=1, source_target_pairs={{0,9},{1,8},{2,11},{3,10},{4,13},{5,12},{6,15},{7,14},{8,1},{9,0},... | collective-permute-start | bytes 98312 | tf_op jit(solution)/shard_map/cond/branch_8_fun/ppermute | solution.py:198
  51.6 4.4 %collective-permute-done.23 = bf16[32,512]{1,0:T(8,128)(2,1)} collective-permute-done((bf16[32,512]{1,0:T(8,128)(2,1)S(1)}, bf16[32,512]{1,0:T(8,128)(2,1)}, u32[]{:S(2)}, u32[]{:S(2)}) %collective-permute-start.23) | collective-permute-done | bytes 32800 | tf_op jit(solution)/shard_map/cond/branch_8_fun/ppermute | solution.py:198
  56.0 2.2 %shard_map.76 = bf16[128,1536]{1,0:T(8,128)(2,1)} custom-call(s32[16]{0:T(128)} %offs_ref.9, s32[16]{0:T(128)} %moved_ref.5, bf16[384,512]{1,0:T(8,128)(2,1)} %get-tuple-element.69.rows_in_ref, bf16[32,512]{1,0:T(8,128)(2,1)} %get-tuple-element.72.answer_ref), custom_call_target="tpu_custom_call" | custom-call | tf_op jit(solution)/shard_map/pallas_call | solution.py:236
  58.1 16.4 %all_to_all.22 = bf16[16,8,1536]{2,1,0:T(8,128)(2,1)} all-to-all(bf16[16,8,1536]{2,1,0:T(8,128)(2,1)} %bitcast.9), channel_id=1, replica_groups=mesh['groups'=2,'req'=16] {'req'}, dimensions={0} | all-to-all | bytes 786432 | tf_op jit(solution)/shard_map/all_to_all | solution.py:239
  74.5 2.3 %shard_map.77 = bf16[48,4096]{1,0:T(8,128)(2,1)} custom-call(s32[1,48]{1,0:T(1,128)} %bitcast.12, s32[16]{0:T(128)} %offs_ref.9, bf16[128,1536]{1,0:T(8,128)(2,1)} %bitcast.10), custom_call_target="tpu_custom_call" | custom-call | tf_op jit(solution)/shard_map/pallas_call | solution.py:240
Async XLA Ops:
  2.4 21.1 %all-to-all-start = ((bf16[16,8,1920]{2,1,0:T(8,128)(2,1)}), bf16[16,8,1920]{2,1,0:T(8,128)(2,1)S(1)}, u32[]{:S(2)}, u32[]{:S(2)}) async-start(bf16[16,8,1920]{2,1,0:T(8,128)(2,1)} %bitcast.8), calls=%async_computation | async-start | bytes 983040 | tf_op jit(solution)/shard_map/all_to_all | solution.py:229
  23.6 0.8 %copy-start = (bf16[16,8,1920]{2,1,0:T(8,128)(2,1)}, bf16[16,8,1920]{2,1,0:T(8,128)(2,1)S(1)}, u32[]{:S(2)}) copy-start(bf16[16,8,1920]{2,1,0:T(8,128)(2,1)S(1)} %all-to-all-done) | copy-start | bytes 1474564
  25.7 5.1 %collective-permute-start.8 = (bf16[32,640]{1,0:T(8,128)(2,1)S(1)}, bf16[32,640]{1,0:T(8,128)(2,1)}, u32[]{:S(2)}, u32[]{:S(2)}) collective-permute-start(bf16[32,640]{1,0:T(8,128)(2,1)S(1)} %param.8), channel_id=1, source_target_pairs={{0,9},{1,8},{2,11},{3,10},{4,13},{5,12},{6,15},{7,14},{8,1},{9,0},... | collective-permute-start | bytes 122888 | tf_op jit(solution)/shard_map/cond/branch_8_fun/ppermute | solution.py:198
  50.6 5.3 %collective-permute-start.23 = (bf16[32,512]{1,0:T(8,128)(2,1)S(1)}, bf16[32,512]{1,0:T(8,128)(2,1)}, u32[]{:S(2)}, u32[]{:S(2)}) collective-permute-start(bf16[32,512]{1,0:T(8,128)(2,1)S(1)} %param.23), channel_id=1, source_target_pairs={{0,9},{1,8},{2,11},{3,10},{4,13},{5,12},{6,15},{7,14},{8,1},{9,0},... | collective-permute-start | bytes 98312 | tf_op jit(solution)/shard_map/cond/branch_8_fun/ppermute | solution.py:198

commit v2 on v1

v2 whole, which is shorter than its diff:
```python
import functools

import jax
import jax.numpy as jnp
from jax import lax
from jax.experimental import pallas as pl
from jax.experimental.pallas import tpu as pltpu
from jax.sharding import PartitionSpec as P

HD = 128
DRAFT = 4
PAGE = 128
R_DEV = 12
PPR = 3
QW = 4096
KVW = 512
KVH = KVW // HD
GRP = QW // KVW
LANES = 128
WIDE = QW // GRP + LANES
SPAN = R_DEV * GRP * DRAFT
SLOT = GRP * DRAFT
LAG = 24
BF = jnp.bfloat16
F32 = jnp.float32
I32 = jnp.int32
VMEM = pl.BlockSpec(memory_space=pltpu.VMEM)
SMEM = pl.BlockSpec(memory_space=pltpu.SMEM)


def iota(shape, dim):
    return lax.broadcasted_iota(I32, shape, dim)


def onehot(mask):
    return jnp.where(mask, jnp.float32(1), jnp.float32(0)).astype(BF)


def exact_dot(a, b):
    return jnp.dot(a, b, preferred_element_type=F32)


def stacked(value, cap):
    width = value.shape[1] // cap
    return jnp.concatenate([value[:, r * width : (r + 1) * width] for r in range(cap)], axis=0)


def wrapped(value, count):
    value = jnp.where(value < 0, value + count, value)
    return jnp.where(value >= count, value - count, value)


def peers_of(k, offs_ref, cap, sign, me, count):
    off = jnp.full(k.shape, offs_ref[0], I32)
    first = jnp.zeros(k.shape, I32)
    for i in range(1, offs_ref.shape[0]):
        off = jnp.where(k >= i * cap, offs_ref[i], off)
        first = jnp.where(k >= i * cap, i * cap, first)
    return wrapped(me + sign * off, count), k - first


def owner_row(index):
    return (index >> 5) * DRAFT + (index & (DRAFT - 1)), (index >> 2) & (GRP - 1)


def pack_kernel(count, cap, order_ref, offs_ref, rows_ref, out_ref, stack_ref):
    rows = rows_ref.shape[0]
    me = lax.axis_index("req")
    peer, place = peers_of(order_ref[...], offs_ref, cap, -1, me, count)
    wide = GRP * rows
    lane = iota((1, wide), 1)
    part = sum([(lane >= h * rows).astype(I32) for h in range(1, GRP)])
    tile = onehot(iota((rows, wide), 0) == lane - part * rows)
    both = jnp.where(iota((8, rows), 0) == 0, peer, place)
    both = exact_dot(both.astype(F32).astype(BF), tile).astype(I32)
    spot = both[:1] * GRP + part
    place = both[1:2]
    for h in range(GRP):
        for g in range(KVH):
            c = (g * GRP + h) * HD
            stack_ref[h * rows : (h + 1) * rows, g * HD : (g + 1) * HD] = rows_ref[:, c : c + HD]
        c = QW + h * HD
        stack_ref[h * rows : (h + 1) * rows, KVH * HD :] = rows_ref[:, c : c + HD]
    at = iota((count * GRP, wide), 0)
    for r in range(cap):
        here = jnp.where(place == r, spot, -1)
        out_ref[:, r * WIDE : (r + 1) * WIDE] = exact_dot(onehot(at == here), stack_ref[...]).astype(BF)


def maps_kernel(
    count,
    cap,
    order_ref,
    offs_ref,
    moved_ref,
    lengths_ref,
    visit_ref,
    take_ref,
    fresh_ref,
    give_ref,
    done_ref,
    limit_ref,
):
    me = lax.axis_index("req")
    moved = moved_ref[me]
    wide = cap * count * GRP
    row = iota((SLOT, wide), 0)
    spot = jnp.zeros((SLOT, wide), I32)
    for t in range(DRAFT):
        k = moved * DRAFT + t
        c = k // cap
        peer = wrapped(me + offs_ref[c], count)
        spot = jnp.where((row & (DRAFT - 1)) == t, (k - c * cap) * (count * GRP) + peer * GRP, spot)
    visit_ref[...] = onehot(iota((SLOT, wide), 1) == spot + (row >> 2))
    row = iota((SPAN, LANES), 0)
    lane = iota((SPAN, LANES), 1)
    fresh = R_DEV * DRAFT
    part = sum([(row >= h * fresh).astype(I32) for h in range(1, GRP)])
    for out, (k, h) in ((take_ref, owner_row(row)), (fresh_ref, (row - part * fresh, part))):
        peer, place = peers_of(k, offs_ref, cap, 1, me, count)
        spot = place * (count * GRP) + peer * GRP + h
        spot = jnp.where((k >> 2) == moved, wide + h * DRAFT + (k & (DRAFT - 1)), spot)
        for b in range(wide // LANES):
            out[:, b * LANES : (b + 1) * LANES] = onehot(spot - b * LANES == lane)
        out[:, wide:] = onehot(spot - wide == lane)[:, :SLOT]
    lane = iota((1, SPAN), 1)
    k, h = owner_row(lane)
    peer, place = peers_of(k, offs_ref, cap, 1, me, count)
    spot = place * (count * GRP) + peer * GRP + h
    at = iota((wide, SPAN), 0)
    give_ref[:, :SPAN] = onehot(at == jnp.where((lane >> 5) == moved, -1, spot))
    lane = iota((1, SLOT), 1)
    spot = jnp.full((1, SLOT), 0, I32)
    for t in range(DRAFT):
        k = moved * DRAFT + t
        c = k // cap
        peer = wrapped(me + offs_ref[c], count)
        spot = jnp.where((lane & (DRAFT - 1)) == t, (k - c * cap) * (count * GRP) + peer * GRP, spot)
    give_ref[:, SPAN:] = onehot(iota((wide, SLOT), 0) == spot + (lane >> 2))
    rows = order_ref.shape[1]
    peer, place = peers_of(order_ref[...], offs_ref, cap, -1, me, count)
    spot = place * (count * GRP) + peer * GRP
    same = iota((rows, rows), 0) == iota((rows, rows), 1)
    spot = jnp.sum(jnp.where(same, spot, 0).astype(F32), axis=1, keepdims=True).astype(I32)
    lane = iota((rows, wide), 1)
    for h in range(GRP):
        done_ref[h * rows : (h + 1) * rows, :] = onehot(lane == spot + h)
    row = iota((16, LANES), 0)
    limit = jnp.full((16, LANES), moved, I32)
    for s in range(R_DEV):
        limit = jnp.where(row == s, lengths_ref[me * R_DEV + s], limit)
    limit_ref[...] = limit


def visitor_kernel(count, cap, visit_ref, in_ref, out_ref):
    out_ref[...] = exact_dot(visit_ref[...], stacked(in_ref[...], cap)).astype(BF)


def attend_kernel(
    count,
    cap,
    take_ref,
    fresh_map_ref,
    limit_ref,
    in_ref,
    visitor_ref,
    cache_ref,
    out_ref,
    answer_ref,
    rows_ref,
    fresh_ref,
    kv_ref,
    score_ref,
    weight_ref,
    inverse_ref,
    sems,
):
    fetches = [
        pltpu.make_async_copy(cache_ref.at[s * PPR : (s + 1) * PPR], kv_ref.at[s * PPR : (s + 1) * PPR], sems.at[s])
        for s in range(R_DEV)
    ]
    for fetch in fetches:
        fetch.start()
    moved = pl.multiple_of(jnp.max(limit_ref[R_DEV : R_DEV + 1, :]) * SLOT, SLOT)
    arrived = jnp.concatenate([stacked(in_ref[...], cap), visitor_ref[...]], axis=0)
    fresh_ref[...] = exact_dot(fresh_map_ref[...], arrived[:, KVW:]).astype(BF)
    rows_ref[...] = exact_dot(take_ref[...], arrived[:, :KVW]).astype(BF)
    fresh = R_DEV * DRAFT
    scale = jnp.float32(HD**-0.5 * 1.4426950408889634)
    span = PPR * PAGE
    contract = (((1,), (1,)), ((), ()))
    position = iota((1, span), 1)
    two = 2 * SLOT
    lane = iota((two, fresh), 1)
    draft = iota((two, fresh), 0) & (DRAFT - 1)
    seen = jnp.where((lane & (DRAFT - 1)) <= draft, lane >> 2, -1)
    low = jnp.float32(-1e30)
    blank = jnp.zeros((SLOT, HD), BF)
    units = [(s, g) for s in range(R_DEV) for g in range(0, KVH, 2)]

    def pair(s, g, kind):
        news = [fresh_ref[(kind * KVH + i) * fresh : (kind * KVH + i + 1) * fresh] for i in (g, g + 1)]
        return jnp.concatenate(
            [kv_ref[s * PPR + p, kind, :, g * HD : (g + 2) * HD] for p in range(PPR)] + [jnp.concatenate(news, axis=1)],
            axis=0,
        )

    def score(u):
        s, g = units[u]
        if g == 0:
            fetches[s].wait()
        mine = slice(s * SLOT, (s + 1) * SLOT)
        first = jnp.concatenate([rows_ref[mine, g * HD : (g + 1) * HD], blank], axis=1)
        second = jnp.concatenate([blank, rows_ref[mine, (g + 1) * HD : (g + 2) * HD]], axis=1)
        queries = jnp.concatenate([first, second], axis=0)
        score_ref[u, :, : span + fresh] = lax.dot_general(
            queries, pair(s, g, 0), contract, preferred_element_type=F32
        )

    def weigh(u):
        s, g = units[u]
        limit = limit_ref[s : s + 1, :]
        limit = jnp.concatenate([limit] * (span // LANES), axis=1)
        old = jnp.where(position < limit, score_ref[u, :, :span], low)
        new = jnp.where(seen == s, score_ref[u, :, span : span + fresh], low)
        peak = jnp.maximum(jnp.max(old, axis=1, keepdims=True), jnp.max(new, axis=1, keepdims=True))
        old = jnp.exp2((old - peak) * scale)
        new = jnp.exp2((new - peak) * scale)
        total = jnp.sum(old, axis=1, keepdims=True) + jnp.sum(new, axis=1, keepdims=True)
        weight_ref[u, :, :span] = old.astype(BF)
        weight_ref[u, :, span : span + fresh] = new.astype(BF)
        inverse_ref[u] = jnp.broadcast_to(1.0 / total, (two, HD))

    def combine(u):
        s, g = units[u]
        mine = slice(s * SLOT, (s + 1) * SLOT)
        summed = exact_dot(weight_ref[u, :, : span + fresh], pair(s, g, 1))
        for i in range(2):
            part = slice(i * SLOT, (i + 1) * SLOT)
            out_ref[mine, (g + i) * HD : (g + i + 1) * HD] = (
                summed[part, i * HD : (i + 1) * HD] * inverse_ref[u, part, :]
            ).astype(BF)

    for i in range(len(units) + LAG + LAG):
        for step, stage in enumerate((score, weigh, combine)):
            if 0 <= i - step * LAG < len(units):
                stage(i - step * LAG)
    answer_ref[...] = out_ref[pl.ds(moved, SLOT), :]


def reply_kernel(count, cap, give_ref, rows_ref, answer_ref, out_ref):
    rows = jnp.concatenate([rows_ref[...], answer_ref[...]], axis=0)
    sent = exact_dot(give_ref[...], rows).astype(BF)
    for r in range(cap):
        out_ref[:, r * KVW : (r + 1) * KVW] = sent[r * count * GRP : (r + 1) * count * GRP]


def finish_kernel(count, cap, done_ref, in_ref, out_ref):
    rows = out_ref.shape[0]
    result = exact_dot(done_ref[...], stacked(in_ref[...], cap)).astype(BF)
    for h in range(GRP):
        for g in range(KVH):
            c = (g * GRP + h) * HD
            out_ref[:, c : c + HD] = result[h * rows : (h + 1) * rows, g * HD : (g + 1) * HD]


def hop(value, mask, count):
    step = 1
    while step < count:
        choices = min(16, count // step)
        digit = jnp.bitwise_and(mask // step, choices - 1)
        only = choices == count
        branches = [
            functools.partial(
                lambda by, v: lax.ppermute(v, "req", [(i, i ^ by) for i in range(count)]), d * step
            )
            for d in range(1, choices)
        ]
        if only:
            value = lax.switch(digit - 1, branches, value)
        else:
            value = lax.switch(digit, [lambda v: v] + branches, value)
        step *= choices
    return value


def on_device(kv_cache, draft_rows, cache_lengths, row_offsets, draft_order, pair_mask, moved_slots):
    count = lax.axis_size("req")
    rows = draft_rows.shape[0]
    cap = max(1, rows // count)
    order = draft_order.reshape(1, rows)
    mask = pair_mask[0]

    def call(kernel, specs, outs, scratch=(), room=8, flops=10**8):
        outs = [o if isinstance(o, jax.ShapeDtypeStruct) else jax.ShapeDtypeStruct(o, BF) for o in outs]
        single = len(outs) == 1
        return pl.pallas_call(
            functools.partial(kernel, count, cap),
            in_specs=specs,
            out_specs=VMEM if single else [VMEM] * len(outs),
            out_shape=outs[0] if single else outs,
            scratch_shapes=[pltpu.VMEM(s, BF) if isinstance(s, tuple) else s for s in scratch],
            compiler_params=pltpu.CompilerParams(vmem_limit_bytes=room * 2**20),
            cost_estimate=pl.CostEstimate(flops=flops, bytes_accessed=10**6, transcendentals=0),
        )

    wide = cap * count * GRP
    outgoing = call(pack_kernel, [VMEM, SMEM, VMEM], [(count * GRP, cap * WIDE)], [(GRP * rows, WIDE)], room=56)(
        order, row_offsets, draft_rows
    )
    incoming = lax.all_to_all(outgoing, "req", split_axis=0, concat_axis=0, tiled=True)
    visit, take, fresh, give, done, limit = call(
        maps_kernel,
        [VMEM, SMEM, SMEM, SMEM],
        [
            (SLOT, wide),
            (SPAN, wide + SLOT),
            (SPAN, wide + SLOT),
            (wide, SPAN + SLOT),
            (GRP * rows, wide),
            jax.ShapeDtypeStruct((16, LANES), I32),
        ],
        room=20,
        flops=10**9,
    )(order, row_offsets, moved_slots, cache_lengths)
    visitor = call(visitor_kernel, [VMEM, VMEM], [(SLOT, WIDE)])(visit, incoming)
    visitor = hop(visitor, mask, count)
    units = R_DEV * KVH // 2
    results, answer = call(
        attend_kernel,
        [VMEM] * 5 + [pl.BlockSpec(memory_space=pltpu.HBM)],
        [(SPAN, KVW), (SLOT, KVW)],
        [
            (SPAN, KVW),
            (SPAN, HD),
            kv_cache.shape,
            pltpu.VMEM((units, 2 * SLOT, (PPR + 1) * PAGE), F32),
            pltpu.VMEM((units, 2 * SLOT, (PPR + 1) * PAGE), BF),
            pltpu.VMEM((units, 2 * SLOT, HD), F32),
            pltpu.SemaphoreType.DMA((R_DEV,)),
        ],
        room=48,
    )(take, fresh, limit, incoming, visitor, kv_cache)
    answer = hop(answer, mask, count)
    backward = call(reply_kernel, [VMEM] * 3, [(count * GRP, cap * KVW)])(give, results, answer)
    returned = lax.all_to_all(backward, "req", split_axis=0, concat_axis=0, tiled=True)
    return call(finish_kernel, [VMEM] * 2, [(rows, QW)])(done, returned)


def solution(mesh):
    in_specs = (
        P(("groups", "req"), None, None, None),
        P(("groups", "req"), None),
        P("groups"),
        P("groups"),
        P(("groups", "req")),
        P("groups"),
        P("groups"),
    )
    out_specs = P(("groups", "req"), None)
    return jax.shard_map(
        on_device, mesh=mesh, in_specs=in_specs, out_specs=out_specs, check_vma=False
    )
```

time: 77.2 us -> 61.9 us (0.80); the launches traced: 76.8 us -> 62.6 us
  Pallas kernels: 28 us -> 13.7 us
  waiting for transfers between devices: 21.2 us -> 16.7 us
  starting transfers between devices: 9.65 us -> 12.7 us
  local copies, waits for them, and re-layouts: 0.77 us -> 2.64 us
    pallas_call x4 -> x5, Pallas kernels: 25.6 us -> 11.3 us  [the longest x1 6.83 us: on_device(): call(attend_kernel, [VMEM] * 5 + [pl.BlockSpec(memory_space=pltpu.HBM)],...]
    all_to_all x1, waiting for transfers between devices: 13.1 us -> 8.44 us  [on_device(): lax.all_to_all(outgoing, 'req', split_axis=0, concat_axis=0, tiled=True)]
    ppermute x2, starting transfers between devices: 2.27 us -> 5.34 us  [hop(): lax.ppermute(v, 'req', [(i, i ^ by) for i in range(count)])]
    unnamed x2 -> x8, local copies, waits for them, and re-layouts: 0.77 us -> 2.64 us
  transfers between devices with their start and end apart: 3 -> 3, of which waited for: 3 -> 3; matrix products, arithmetic and copies ran while one was open for 0% -> 0% of each run, Pallas kernels for 0% -> 3%
where the time goes in v2:
time: 61.9 us; the launch traced here: 62.6 us
  waiting for transfers between devices  16.7 us (27%)
  blocking collectives  15.9 us (26%)
  Pallas kernels  13.7 us (22%)
  starting transfers between devices  12.7 us (21%)
  local copies, waits for them, and re-layouts  2.64 us (4%)
  between operations  0.7 us (1%)
    all_to_all x1, blocking collectives, on_device(): lax.all_to_all(backward, 'req', split_axis=0, concat_axis=0, tiled=True)  15.9 us
    all_to_all x1, waiting for transfers between devices, on_device(): lax.all_to_all(outgoing, 'req', split_axis=0, concat_axis=0, tiled=True)  8.44 us
    ppermute x2, waiting for transfers between devices, hop(): lax.ppermute(v, 'req', [(i, i ^ by) for i in range(count)])  8.31 us
    all_to_all x1, starting transfers between devices, on_device(): lax.all_to_all(outgoing, 'req', split_axis=0, concat_axis=0, tiled=True)  7.39 us
    pallas_call x1, Pallas kernels, on_device(): call(attend_kernel, [VMEM] * 5 + [pl.BlockSpec(memory_space=pltpu.HBM)],...  6.83 us
    ppermute x2, starting transfers between devices, hop(): lax.ppermute(v, 'req', [(i, i ^ by) for i in range(count)])  5.34 us
    unnamed x8, local copies, waits for them, and re-layouts  2.64 us
    pallas_call x1, Pallas kernels, on_device(): call(pack_kernel, [VMEM, SMEM, VMEM], [(count * GRP, cap * WIDE)], [(GRP...  2.45 us
  transfers between devices with their start and end apart: 3, of which 3 were waited for; matrix products, arithmetic and copies ran while one was open for 0% of the time, Pallas kernels for 3%

profile of v2, /device:TPU:0, one launch (start us, length us, event | category | flops | bytes accessed | tf_op | source)
XLA Modules:
  0.0 62.6 jit_solution(5761396144708306947)
XLA Ops:
  0.0 2.4 %shard_map.74 = bf16[128,1920]{1,0:T(8,128)(2,1)} custom-call(s32[1,48]{1,0:T(1,128)} %bitcast.10, s32[16]{0:T(128)} %offs_ref.3, bf16[48,5120]{1,0:T(8,128)(2,1)} %rows_ref.1), custom_call_target="tpu_custom_call" | custom-call | flops 100000000 | bytes 1000000 | tf_op jit(solution)/shard_map/pallas_call | solution.py:308
  2.5 7.4 %all-to-all-start = ((bf16[16,8,1920]{2,1,0:T(8,128)(2,1)}), bf16[16,8,1920]{2,1,0:T(8,128)(2,1)S(1)}, u32[]{:S(2)}, u32[]{:S(2)}) async-start(bf16[16,8,1920]{2,1,0:T(8,128)(2,1)} %bitcast.12), calls=%async_computation | async-start | bytes 983040 | tf_op jit(solution)/shard_map/all_to_all | solution.py:311
  10.5 0.0 copy-start
  10.5 0.6 %copy-done = s32[48]{0:T(128)S(1)} copy-done((s32[48]{0:T(128)S(1)}, s32[48]{0:T(128)}, u32[]{:S(2)}) %copy-start) | copy-done | bytes 216
  11.2 0.0 copy-start.1
  11.2 0.7 %copy-done.1 = s32[16]{0:T(128)S(1)} copy-done((s32[16]{0:T(128)S(1)}, s32[16]{0:T(128)}, u32[]{:S(2)}) %copy-start.1) | copy-done | bytes 88
  11.8 0.0 copy-start.2
  11.8 0.7 %copy-done.2 = s32[192]{0:T(256)S(1)} copy-done((s32[192]{0:T(256)S(1)}, s32[192]{0:T(256)}, u32[]{:S(2)}) %copy-start.2) | copy-done | bytes 792
  12.5 0.0 copy-start.3
  12.5 0.7 %copy-done.3 = s32[16]{0:T(128)S(1)} copy-done((s32[16]{0:T(128)S(1)}, s32[16]{0:T(128)}, u32[]{:S(2)}) %copy-start.3) | copy-done | bytes 88
  13.1 2.0 %shard_map.73 = (bf16[32,384]{1,0:T(8,128)(2,1)S(1)}, bf16[384,416]{1,0:T(8,128)(2,1)S(1)}, bf16[384,416]{1,0:T(8,128)(2,1)S(1)}, bf16[384,416]{1,0:T(8,128)(2,1...) custom-call(s32[1,48]{1,0:T(1,128)S(1)} %bitcast.11, s32[16]{0:T(128)S(1)} %copy-done.1, s32[16]{0:T(128)S(1)} %copy-done.3, ...), custom_call_target="tpu_custom_call" | custom-call | flops 1000000000 | bytes 1000000 | tf_op jit(solution)/shard_map/pallas_call | solution.py:312
  15.2 8.4 %all-to-all-done = bf16[16,8,1920]{2,1,0:T(8,128)(2,1)S(1)} async-done(((bf16[16,8,1920]{2,1,0:T(8,128)(2,1)}), bf16[16,8,1920]{2,1,0:T(8,128)(2,1)S(1)}, u32[]{:S(2)}, u32[]{:S(2)}) %all-to-all-start) | async-done | bytes 491552 | tf_op jit(solution)/shard_map/all_to_all | solution.py:311
  23.6 0.2 shard_map.75
  23.8 6.9 %conditional.2 = (bf16[32,640]{1,0:T(8,128)(2,1)}) conditional(s32[]{:T(128)} %bitcast.3, bf16[32,640]{1,0:T(8,128)(2,1)S(1)} %shard_map.75, bf16[32,640]{1,0:T(8,128)(2,1)S(1)} %shard_map.75, bf16[32,640]{1,0:T(8,128)(2,1)S(1)} %shard_map.75, bf16[32,640]{1,0:T(8,128)(2,1)S(1)} %shard_map.75, ...), branch_computations={%region_0.1_spmd, %region_1.2_spmd, %region_2.3_spmd, %region_3.4_... | conditional | bytes 163888 | solution.py:280
  23.8 2.7 %collective-permute-start.13 = (bf16[32,640]{1,0:T(8,128)(2,1)S(1)}, bf16[32,640]{1,0:T(8,128)(2,1)}, u32[]{:S(2)}, u32[]{:S(2)}) collective-permute-start(bf16[32,640]{1,0:T(8,128)(2,1)S(1)} %param.13), channel_id=1, source_target_pairs={{0,14},{1,15},{2,12},{3,13},{4,10},{5,11},{6,8},{7,9},{8,6},{9,7},... | collective-permute-start | bytes 122888 | tf_op jit(solution)/shard_map/cond/branch_13_fun/ppermute | solution.py:275
  26.5 4.2 %collective-permute-done.13 = bf16[32,640]{1,0:T(8,128)(2,1)} collective-permute-done((bf16[32,640]{1,0:T(8,128)(2,1)S(1)}, bf16[32,640]{1,0:T(8,128)(2,1)}, u32[]{:S(2)}, u32[]{:S(2)}) %collective-permute-start.13) | collective-permute-done | bytes 40992 | tf_op jit(solution)/shard_map/cond/branch_13_fun/ppermute | solution.py:275
  30.7 6.8 %shard_map.76 = (bf16[384,512]{1,0:T(8,128)(2,1)S(1)}, bf16[32,512]{1,0:T(8,128)(2,1)S(1)}) custom-call(bf16[384,416]{1,0:T(8,128)(2,1)S(1)} %get-tuple-element.77.take_ref, bf16[384,416]{1,0:T(8,128)(2,1)S(1)} %get-tuple-element.78.fresh_map_ref, s32[16,128]{1,0:T(8,128)S(1)} %get-tuple-element.79.limit_ref, bf16[128,1920]{1,0:T(8,128)(2,1)S(1)} %bitcast.7, ...), custom_call_target="tpu_custom_call" | custom-call | flops 100000000 | bytes 1000000 | tf_op jit(solution)/shard_map/pallas_call | solution.py:329
  37.5 6.8 %conditional.3 = (bf16[32,512]{1,0:T(8,128)(2,1)}) conditional(s32[]{:T(128)} %bitcast.3, bf16[32,512]{1,0:T(8,128)(2,1)S(1)} %get-tuple-element.82, bf16[32,512]{1,0:T(8,128)(2,1)S(1)} %get-tuple-element.82, bf16[32,512]{1,0:T(8,128)(2,1)S(1)} %get-tuple-element.82, ...), branch_computations={%region_15.16_spmd, %region_16.17_spmd, %region_17.18_spmd, %regio... | conditional | bytes 131120 | solution.py:280
  37.6 2.7 %collective-permute-start.28 = (bf16[32,512]{1,0:T(8,128)(2,1)S(1)}, bf16[32,512]{1,0:T(8,128)(2,1)}, u32[]{:S(2)}, u32[]{:S(2)}) collective-permute-start(bf16[32,512]{1,0:T(8,128)(2,1)S(1)} %param.28), channel_id=1, source_target_pairs={{0,14},{1,15},{2,12},{3,13},{4,10},{5,11},{6,8},{7,9},{8,6},{9,7},... | collective-permute-start | bytes 98312 | tf_op jit(solution)/shard_map/cond/branch_13_fun/ppermute | solution.py:275
  40.3 4.1 %collective-permute-done.28 = bf16[32,512]{1,0:T(8,128)(2,1)} collective-permute-done((bf16[32,512]{1,0:T(8,128)(2,1)S(1)}, bf16[32,512]{1,0:T(8,128)(2,1)}, u32[]{:S(2)}, u32[]{:S(2)}) %collective-permute-start.28) | collective-permute-done | bytes 32800 | tf_op jit(solution)/shard_map/cond/branch_13_fun/ppermute | solution.py:275
  44.4 1.1 %shard_map.77 = bf16[128,1536]{1,0:T(8,128)(2,1)S(1)} custom-call(bf16[384,416]{1,0:T(8,128)(2,1)S(1)} %get-tuple-element.76.give_ref, bf16[384,512]{1,0:T(8,128)(2,1)S(1)} %get-tuple-element.81.rows_ref, bf16[32,512]{1,0:T(8,128)(2,1)} %get-tuple-element.84.answer_ref), custom_call_target="tpu_custom_call" | custom-call | flops 100000000 | bytes 1000000 | tf_op jit(solution)/shard_map/pallas_call | solution.py:345
  45.5 15.9 %all_to_all.22 = bf16[16,8,1536]{2,1,0:T(8,128)(2,1)S(1)} all-to-all(bf16[16,8,1536]{2,1,0:T(8,128)(2,1)S(1)} %bitcast.9), channel_id=1, replica_groups=mesh['groups'=2,'req'=16] {'req'}, dimensions={0} | all-to-all | bytes 786432 | tf_op jit(solution)/shard_map/all_to_all | solution.py:346
  61.5 1.1 %shard_map.78 = bf16[48,4096]{1,0:T(8,128)(2,1)} custom-call(bf16[384,384]{1,0:T(8,128)(2,1)S(1)} %get-tuple-element.75.done_ref, bf16[128,1536]{1,0:T(8,128)(2,1)S(1)} %bitcast.8), custom_call_target="tpu_custom_call" | custom-call | flops 100000000 | bytes 1000000 | tf_op jit(solution)/shard_map/pallas_call | solution.py:347
Async XLA Ops:
  2.5 21.1 %all-to-all-start = ((bf16[16,8,1920]{2,1,0:T(8,128)(2,1)}), bf16[16,8,1920]{2,1,0:T(8,128)(2,1)S(1)}, u32[]{:S(2)}, u32[]{:S(2)}) async-start(bf16[16,8,1920]{2,1,0:T(8,128)(2,1)} %bitcast.12), calls=%async_computation | async-start | bytes 983040 | tf_op jit(solution)/shard_map/all_to_all | solution.py:311
  10.5 0.7 %copy-start = (s32[48]{0:T(128)S(1)}, s32[48]{0:T(128)}, u32[]{:S(2)}) copy-start(s32[48]{0:T(128)} %param.41) | copy-start | bytes 580
  11.2 0.7 %copy-start.1 = (s32[16]{0:T(128)S(1)}, s32[16]{0:T(128)}, u32[]{:S(2)}) copy-start(s32[16]{0:T(128)} %offs_ref.3) | copy-start | bytes 196
  11.8 0.7 %copy-start.2 = (s32[192]{0:T(256)S(1)}, s32[192]{0:T(256)}, u32[]{:S(2)}) copy-start(s32[192]{0:T(256)} %lengths_ref.1) | copy-start | bytes 2308
  12.5 0.7 %copy-start.3 = (s32[16]{0:T(128)S(1)}, s32[16]{0:T(128)}, u32[]{:S(2)}) copy-start(s32[16]{0:T(128)} %moved_ref.1) | copy-start | bytes 196
  23.8 6.9 %collective-permute-start.13 = (bf16[32,640]{1,0:T(8,128)(2,1)S(1)}, bf16[32,640]{1,0:T(8,128)(2,1)}, u32[]{:S(2)}, u32[]{:S(2)}) collective-permute-start(bf16[32,640]{1,0:T(8,128)(2,1)S(1)} %param.13), channel_id=1, source_target_pairs={{0,14},{1,15},{2,12},{3,13},{4,10},{5,11},{6,8},{7,9},{8,6},{9,7},... | collective-permute-start | bytes 122888 | tf_op jit(solution)/shard_map/cond/branch_13_fun/ppermute | solution.py:275
  37.6 6.8 %collective-permute-start.28 = (bf16[32,512]{1,0:T(8,128)(2,1)S(1)}, bf16[32,512]{1,0:T(8,128)(2,1)}, u32[]{:S(2)}, u32[]{:S(2)}) collective-permute-start(bf16[32,512]{1,0:T(8,128)(2,1)S(1)} %param.28), channel_id=1, source_target_pairs={{0,14},{1,15},{2,12},{3,13},{4,10},{5,11},{6,8},{7,9},{8,6},{9,7},... | collective-permute-start | bytes 98312 | tf_op jit(solution)/shard_map/cond/branch_13_fun/ppermute | solution.py:275

commit v3 on v2

--- a/solution.py
+++ b/solution.py
@@ -20,7 +20,9 @@
 WIDE = QW // GRP + LANES
 SPAN = R_DEV * GRP * DRAFT
 SLOT = GRP * DRAFT
-LAG = 24
+HALF = R_DEV // 2
+BODY = 3
+ROOM = 16
 BF = jnp.bfloat16
 F32 = jnp.float32
 I32 = jnp.int32
@@ -96,7 +98,6 @@
     lengths_ref,
     visit_ref,
     take_ref,
-    fresh_ref,
     give_ref,
     done_ref,
     limit_ref,
@@ -114,15 +115,11 @@
     visit_ref[...] = onehot(iota((SLOT, wide), 1) == spot + (row >> 2))
     row = iota((SPAN, LANES), 0)
     lane = iota((SPAN, LANES), 1)
-    fresh = R_DEV * DRAFT
-    part = sum([(row >= h * fresh).astype(I32) for h in range(1, GRP)])
-    for out, (k, h) in ((take_ref, owner_row(row)), (fresh_ref, (row - part * fresh, part))):
-        peer, place = peers_of(k, offs_ref, cap, 1, me, count)
-        spot = place * (count * GRP) + peer * GRP + h
-        spot = jnp.where((k >> 2) == moved, wide + h * DRAFT + (k & (DRAFT - 1)), spot)
-        for b in range(wide // LANES):
-            out[:, b * LANES : (b + 1) * LANES] = onehot(spot - b * LANES == lane)
-        out[:, wide:] = onehot(spot - wide == lane)[:, :SLOT]
+    k, h = owner_row(row)
+    peer, place = peers_of(k, offs_ref, cap, 1, me, count)
+    spot = place * (count * GRP) + peer * GRP + h
+    for b in range(wide // LANES):
+        take_ref[:, b * LANES : (b + 1) * LANES] = onehot(spot - b * LANES == lane)
     lane = iota((1, SPAN), 1)
     k, h = owner_row(lane)
     peer, place = peers_of(k, offs_ref, cap, 1, me, count)
@@ -147,6 +144,7 @@
         done_ref[h * rows : (h + 1) * rows, :] = onehot(lane == spot + h)
     row = iota((16, LANES), 0)
     limit = jnp.full((16, LANES), moved, I32)
+    limit = jnp.where(row == R_DEV + 1, lengths_ref[me * R_DEV + moved], limit)
     for s in range(R_DEV):
         limit = jnp.where(row == s, lengths_ref[me * R_DEV + s], limit)
     limit_ref[...] = limit
@@ -156,73 +154,41 @@
     out_ref[...] = exact_dot(visit_ref[...], stacked(in_ref[...], cap)).astype(BF)
 
 
-def attend_kernel(
-    count,
-    cap,
-    take_ref,
-    fresh_map_ref,
-    limit_ref,
-    in_ref,
-    visitor_ref,
-    cache_ref,
-    out_ref,
-    answer_ref,
-    rows_ref,
-    fresh_ref,
-    kv_ref,
-    score_ref,
-    weight_ref,
-    inverse_ref,
-    sems,
-):
-    fetches = [
-        pltpu.make_async_copy(cache_ref.at[s * PPR : (s + 1) * PPR], kv_ref.at[s * PPR : (s + 1) * PPR], sems.at[s])
-        for s in range(R_DEV)
-    ]
-    for fetch in fetches:
-        fetch.start()
-    moved = pl.multiple_of(jnp.max(limit_ref[R_DEV : R_DEV + 1, :]) * SLOT, SLOT)
-    arrived = jnp.concatenate([stacked(in_ref[...], cap), visitor_ref[...]], axis=0)
-    fresh_ref[...] = exact_dot(fresh_map_ref[...], arrived[:, KVW:]).astype(BF)
-    rows_ref[...] = exact_dot(take_ref[...], arrived[:, :KVW]).astype(BF)
-    fresh = R_DEV * DRAFT
+def attend(slots, rows_of, pages_of, limit_of, put, score_ref, weight_ref, inverse_ref):
+    span = PPR * PAGE
+    fresh = KVH * DRAFT
+    two = 2 * SLOT
     scale = jnp.float32(HD**-0.5 * 1.4426950408889634)
-    span = PPR * PAGE
-    contract = (((1,), (1,)), ((), ()))
+    low = jnp.float32(-1e30)
     position = iota((1, span), 1)
-    two = 2 * SLOT
     lane = iota((two, fresh), 1)
-    draft = iota((two, fresh), 0) & (DRAFT - 1)
-    seen = jnp.where((lane & (DRAFT - 1)) <= draft, lane >> 2, -1)
-    low = jnp.float32(-1e30)
+    row = iota((two, fresh), 0)
+    seen = jnp.where((lane & (DRAFT - 1)) <= (row & (DRAFT - 1)), (lane >> 2) - (row >> 5), -1)
     blank = jnp.zeros((SLOT, HD), BF)
-    units = [(s, g) for s in range(R_DEV) for g in range(0, KVH, 2)]
+    units = [(s, g) for s in slots for g in range(0, KVH, 2)]
 
     def pair(s, g, kind):
-        news = [fresh_ref[(kind * KVH + i) * fresh : (kind * KVH + i + 1) * fresh] for i in (g, g + 1)]
-        return jnp.concatenate(
-            [kv_ref[s * PPR + p, kind, :, g * HD : (g + 2) * HD] for p in range(PPR)] + [jnp.concatenate(news, axis=1)],
-            axis=0,
-        )
+        new = rows_of(s)[kind * fresh : (kind + 1) * fresh, KVW:]
+        pages = [pages_of(s, p, kind, slice(g * HD, (g + 2) * HD)) for p in range(PPR)]
+        return jnp.concatenate(pages + [jnp.concatenate([new, new], axis=1)], axis=0)
 
     def score(u):
         s, g = units[u]
-        if g == 0:
-            fetches[s].wait()
-        mine = slice(s * SLOT, (s + 1) * SLOT)
-        first = jnp.concatenate([rows_ref[mine, g * HD : (g + 1) * HD], blank], axis=1)
-        second = jnp.concatenate([blank, rows_ref[mine, (g + 1) * HD : (g + 2) * HD]], axis=1)
-        queries = jnp.concatenate([first, second], axis=0)
+        rows = rows_of(s)
+        first = jnp.concatenate([rows[:, g * HD : (g + 1) * HD], blank], axis=1)
+        second = jnp.concatenate([blank, rows[:, (g + 1) * HD : (g + 2) * HD]], axis=1)
         score_ref[u, :, : span + fresh] = lax.dot_general(
-            queries, pair(s, g, 0), contract, preferred_element_type=F32
+            jnp.concatenate([first, second], axis=0),
+            pair(s, g, 0),
+            (((1,), (1,)), ((), ())),
+            preferred_element_type=F32,
         )
 
     def weigh(u):
         s, g = units[u]
-        limit = limit_ref[s : s + 1, :]
-        limit = jnp.concatenate([limit] * (span // LANES), axis=1)
+        limit = jnp.concatenate([limit_of(s)] * (span // LANES), axis=1)
         old = jnp.where(position < limit, score_ref[u, :, :span], low)
-        new = jnp.where(seen == s, score_ref[u, :, span : span + fresh], low)
+        new = jnp.where(seen == g, score_ref[u, :, span : span + fresh], low)
         peak = jnp.maximum(jnp.max(old, axis=1, keepdims=True), jnp.max(new, axis=1, keepdims=True))
         old = jnp.exp2((old - peak) * scale)
         new = jnp.exp2((new - peak) * scale)
@@ -233,23 +199,70 @@
 
     def combine(u):
         s, g = units[u]
-        mine = slice(s * SLOT, (s + 1) * SLOT)
         summed = exact_dot(weight_ref[u, :, : span + fresh], pair(s, g, 1))
         for i in range(2):
             part = slice(i * SLOT, (i + 1) * SLOT)
-            out_ref[mine, (g + i) * HD : (g + i + 1) * HD] = (
-                summed[part, i * HD : (i + 1) * HD] * inverse_ref[u, part, :]
-            ).astype(BF)
-
-    for i in range(len(units) + LAG + LAG):
-        for step, stage in enumerate((score, weigh, combine)):
-            if 0 <= i - step * LAG < len(units):
-                stage(i - step * LAG)
-    answer_ref[...] = out_ref[pl.ds(moved, SLOT), :]
-
-
-def reply_kernel(count, cap, give_ref, rows_ref, answer_ref, out_ref):
-    rows = jnp.concatenate([rows_ref[...], answer_ref[...]], axis=0)
+            put(s, g + i, (summed[part, i * HD : (i + 1) * HD] * inverse_ref[u, part, :]).astype(BF))
+
+    for stage in (score, weigh, combine):
+        for u in range(len(units)):
+            stage(u)
+
+
+def attend_half(low, rows_ref, pages_ref, limit_ref, out_ref, scratch, ready=lambda s: None):
+    def step(i, carry):
+        slots = [i * BODY + j for j in range(BODY)]
+        for s in slots:
+            ready(s)
+
+        def put(s, g, value):
+            out_ref[pl.ds(pl.multiple_of(s * SLOT, SLOT), SLOT), g * HD : (g + 1) * HD] = value
+
+        attend(
+            slots,
+            lambda s: rows_ref[pl.ds(pl.multiple_of((s + low) * SLOT, SLOT), SLOT), :],
+            lambda s, p, kind, cols: pages_ref[s * PPR + p, kind, :, cols],
+            lambda s: limit_ref[pl.ds(s + low, 1), :],
+            put,
+            *scratch,
+        )
+        return carry
+
+    lax.fori_loop(0, HALF // BODY, step, 0)
+
+
+def first_kernel(count, cap, take_ref, limit_ref, in_ref, cache_ref, out_ref, rows_ref, pages_ref, sems, *scratch):
+    def fetch(s):
+        return pltpu.make_async_copy(cache_ref.at[pl.ds(s * PPR, PPR)], pages_ref.at[pl.ds(s * PPR, PPR)], sems.at[s])
+
+    for s in range(HALF):
+        fetch(s).start()
+    rows_ref[...] = exact_dot(take_ref[...], stacked(in_ref[...], cap)).astype(BF)
+    attend_half(0, rows_ref, pages_ref, limit_ref, out_ref, scratch, lambda s: fetch(s).wait())
+
+
+def second_kernel(count, cap, rows_ref, limit_ref, answer_ref, cache_ref, out_ref, *scratch):
+    attend_half(HALF, rows_ref, cache_ref.at[pl.ds(HALF * PPR, HALF * PPR)], limit_ref, out_ref, scratch)
+
+
+def guest_kernel(count, cap, visitor_ref, limit_ref, cache_ref, out_ref, *scratch):
+    moved = jnp.max(limit_ref[R_DEV : R_DEV + 1, :])
+
+    def put(s, g, value):
+        out_ref[:, g * HD : (g + 1) * HD] = value
+
+    attend(
+        [moved],
+        lambda s: visitor_ref[...],
+        lambda s, p, kind, cols: cache_ref[s * PPR + p, kind, :, cols],
+        lambda s: limit_ref[R_DEV + 1 : R_DEV + 2, :],
+        put,
+        *scratch,
+    )
+
+
+def reply_kernel(count, cap, give_ref, first_ref, second_ref, answer_ref, out_ref):
+    rows = jnp.concatenate([first_ref[...], second_ref[...], answer_ref[...]], axis=0)
     sent = exact_dot(give_ref[...], rows).astype(BF)
     for r in range(cap):
         out_ref[:, r * KVW : (r + 1) * KVW] = sent[r * count * GRP : (r + 1) * count * GRP]
@@ -264,24 +277,26 @@
             out_ref[:, c : c + HD] = result[h * rows : (h + 1) * rows, g * HD : (g + 1) * HD]
 
 
-def hop(value, mask, count):
-    step = 1
-    while step < count:
-        choices = min(16, count // step)
-        digit = jnp.bitwise_and(mask // step, choices - 1)
-        only = choices == count
+def through_partner(mask, count, work, *args):
+    def permuted(by, value):
+        return lax.ppermute(value, "req", [(i, i ^ by) for i in range(count)])
+
+    if count <= 16:
         branches = [
-            functools.partial(
-                lambda by, v: lax.ppermute(v, "req", [(i, i ^ by) for i in range(count)]), d * step
-            )
-            for d in range(1, choices)
+            functools.partial(lambda by, *a: work(functools.partial(permuted, by), *a), by) for by in range(1, count)
         ]
-        if only:
-            value = lax.switch(digit - 1, branches, value)
-        else:
-            value = lax.switch(digit, [lambda v: v] + branches, value)
-        step *= choices
-    return value
+        return lax.switch(mask - 1, branches, *args)
+
+    def swap(value):
+        step = 1
+        while step < count:
+            choices = min(16, count // step)
+            branches = [lambda v: v] + [functools.partial(permuted, d * step) for d in range(1, choices)]
+            value = lax.switch(jnp.bitwise_and(mask // step, choices - 1), branches, value)
+            step *= choices
+        return value
+
+    return work(swap, *args)
 
 
 def on_device(kv_cache, draft_rows, cache_lengths, row_offsets, draft_order, pair_mask, moved_slots):
@@ -309,13 +324,12 @@
         order, row_offsets, draft_rows
     )
     incoming = lax.all_to_all(outgoing, "req", split_axis=0, concat_axis=0, tiled=True)
-    visit, take, fresh, give, done, limit = call(
+    visit, take, give, done, limit = call(
         maps_kernel,
         [VMEM, SMEM, SMEM, SMEM],
         [
             (SLOT, wide),
-            (SPAN, wide + SLOT),
-            (SPAN, wide + SLOT),
+            (SPAN, wide),
             (wide, SPAN + SLOT),
             (GRP * rows, wide),
             jax.ShapeDtypeStruct((16, LANES), I32),
@@ -324,25 +338,34 @@
         flops=10**9,
     )(order, row_offsets, moved_slots, cache_lengths)
     visitor = call(visitor_kernel, [VMEM, VMEM], [(SLOT, WIDE)])(visit, incoming)
-    visitor = hop(visitor, mask, count)
-    units = R_DEV * KVH // 2
-    results, answer = call(
-        attend_kernel,
-        [VMEM] * 5 + [pl.BlockSpec(memory_space=pltpu.HBM)],
-        [(SPAN, KVW), (SLOT, KVW)],
-        [
-            (SPAN, KVW),
-            (SPAN, HD),
-            kv_cache.shape,
-            pltpu.VMEM((units, 2 * SLOT, (PPR + 1) * PAGE), F32),
-            pltpu.VMEM((units, 2 * SLOT, (PPR + 1) * PAGE), BF),
-            pltpu.VMEM((units, 2 * SLOT, HD), F32),
-            pltpu.SemaphoreType.DMA((R_DEV,)),
-        ],
-        room=48,
-    )(take, fresh, limit, incoming, visitor, kv_cache)
-    answer = hop(answer, mask, count)
-    backward = call(reply_kernel, [VMEM] * 3, [(count * GRP, cap * KVW)])(give, results, answer)
+    def units(slots):
+        return [
+            pltpu.VMEM((slots * KVH // 2, 2 * SLOT, (PPR + 1) * PAGE), F32),
+            pltpu.VMEM((slots * KVH // 2, 2 * SLOT, (PPR + 1) * PAGE), BF),
+            pltpu.VMEM((slots * KVH // 2, 2 * SLOT, HD), F32),
+        ]
+
+    hbm = pl.BlockSpec(memory_space=pltpu.HBM)
+    pages = (HALF * PPR,) + kv_cache.shape[1:]
+
+    def work(swap, visitor, take, give, limit, incoming, kv_cache):
+        arrived = swap(visitor)
+        first, owned = call(
+            first_kernel,
+            [VMEM] * 3 + [hbm],
+            [(HALF * SLOT, KVW), (SPAN, WIDE)],
+            [pages, pltpu.SemaphoreType.DMA((HALF,))] + units(BODY),
+            room=ROOM,
+            flops=2 * 10**9,
+        )(take, limit, incoming, kv_cache)
+        answer = call(guest_kernel, [VMEM] * 3, [(SLOT, KVW)], units(1), room=16)(arrived, limit, kv_cache)
+        second = call(
+            second_kernel, [VMEM] * 4, [(HALF * SLOT, KVW)], units(BODY), room=16, flops=2 * 10**9
+        )(owned, limit, answer, kv_cache)
+        answer = swap(answer)
+        return call(reply_kernel, [VMEM] * 4, [(count * GRP, cap * KVW)])(give, first, second, answer)
+
+    backward = through_partner(mask, count, work, visitor, take, give, limit, incoming, kv_cache)
     returned = lax.all_to_all(backward, "req", split_axis=0, concat_axis=0, tiled=True)
     return call(finish_kernel, [VMEM] * 2, [(rows, QW)])(done, returned)
 

time: 61.9 us -> 52.7 us (0.85)
  waiting for transfers between devices: 16.7 us -> 11 us
  starting transfers between devices: 12.7 us -> 10.3 us
  Pallas kernels: 13.7 us -> 12 us
  loops' own time: 0.1 us -> 0.81 us
    ppermute x2, waiting for transfers between devices: 8.31 us -> 2.13 us  [permuted(): return lax.ppermute(value, 'req', [(i, i ^ by) for i in range(count)])]
    ppermute x2, starting transfers between devices: 5.34 us -> 2.89 us  [permuted(): return lax.ppermute(value, 'req', [(i, i ^ by) for i in range(count)])]
    pallas_call x3 -> x5, Pallas kernels: 9.95 us -> 8.17 us  [the longest x1 3.99 us: work(): call(first_kernel, [VMEM] * 3 + [hbm], [(HALF * SLOT, KVW), (SPAN, WIDE)]...]
    another operation x2 -> x1, loops' own time: 0.1 us -> 0.81 us  [through_partner(): return lax.switch(mask - 1, branches, *args)]
  transfers between devices with their start and end apart: 3 -> 3, of which waited for: 3 -> 2; matrix products, arithmetic and copies ran while one was open for 0% -> 0% of each run, Pallas kernels for 3% -> 13%
where the time goes in v3:
time: 52.7 us; the launch traced here: 53.6 us
  blocking collectives  16.2 us (31%)
  Pallas kernels  12 us (23%)
  waiting for transfers between devices  11 us (21%)
  starting transfers between devices  10.3 us (20%)
  local copies, waits for them, and re-layouts  2.64 us (5%)
  loops' own time  0.81 us (2%)
  between operations  0.7 us (1%)
    all_to_all x1, blocking collectives, on_device(): lax.all_to_all(backward, 'req', split_axis=0, concat_axis=0, tiled=True)  16.2 us
    all_to_all x1, waiting for transfers between devices, on_device(): lax.all_to_all(outgoing, 'req', split_axis=0, concat_axis=0, tiled=True)  8.89 us
    all_to_all x1, starting transfers between devices, on_device(): lax.all_to_all(outgoing, 'req', split_axis=0, concat_axis=0, tiled=True)  7.41 us
    pallas_call x1, Pallas kernels, work(): call(first_kernel, [VMEM] * 3 + [hbm], [(HALF * SLOT, KVW), (SPAN, WIDE)]...  3.99 us
    ppermute x2, starting transfers between devices, permuted(): return lax.ppermute(value, 'req', [(i, i ^ by) for i in range(count)])  2.89 us
    unnamed x8, local copies, waits for them, and re-layouts  2.64 us
    pallas_call x1, Pallas kernels, on_device(): call(pack_kernel, [VMEM, SMEM, VMEM], [(count * GRP, cap * WIDE)], [(GRP...  2.48 us
    ppermute x2, waiting for transfers between devices, permuted(): return lax.ppermute(value, 'req', [(i, i ^ by) for i in range(count)])  2.13 us
  transfers between devices with their start and end apart: 3, of which 2 were waited for; matrix products, arithmetic and copies ran while one was open for 0% of the time, Pallas kernels for 13%

profile of v3, /device:TPU:0, one launch (start us, length us, event | category | flops | bytes accessed | tf_op | source)
XLA Modules:
  0.0 53.6 jit_solution(15021973772303667787)
XLA Ops:
  0.0 2.5 %shard_map.74 = bf16[128,1920]{1,0:T(8,128)(2,1)} custom-call(s32[1,48]{1,0:T(1,128)} %bitcast.7, s32[16]{0:T(128)} %offs_ref.3, bf16[48,5120]{1,0:T(8,128)(2,1)} %rows_ref.1), custom_call_target="tpu_custom_call" | custom-call | flops 100000000 | bytes 1000000 | tf_op jit(solution)/shard_map/pallas_call | solution.py:323
  2.5 7.4 %all-to-all-start = ((bf16[16,8,1920]{2,1,0:T(8,128)(2,1)}), bf16[16,8,1920]{2,1,0:T(8,128)(2,1)S(1)}, u32[]{:S(2)}, u32[]{:S(2)}) async-start(bf16[16,8,1920]{2,1,0:T(8,128)(2,1)} %bitcast.25), calls=%async_computation | async-start | bytes 983040 | tf_op jit(solution)/shard_map/all_to_all | solution.py:326
  10.5 0.0 copy-start
  10.6 0.6 %copy-done = s32[48]{0:T(128)S(1)} copy-done((s32[48]{0:T(128)S(1)}, s32[48]{0:T(128)}, u32[]{:S(2)}) %copy-start) | copy-done | bytes 216
  11.2 0.0 copy-start.1
  11.2 0.7 %copy-done.1 = s32[16]{0:T(128)S(1)} copy-done((s32[16]{0:T(128)S(1)}, s32[16]{0:T(128)}, u32[]{:S(2)}) %copy-start.1) | copy-done | bytes 88
  11.9 0.0 copy-start.2
  11.9 0.7 %copy-done.2 = s32[192]{0:T(256)S(1)} copy-done((s32[192]{0:T(256)S(1)}, s32[192]{0:T(256)}, u32[]{:S(2)}) %copy-start.2) | copy-done | bytes 792
  12.5 0.0 copy-start.3
  12.5 0.7 %copy-done.3 = s32[16]{0:T(128)S(1)} copy-done((s32[16]{0:T(128)S(1)}, s32[16]{0:T(128)}, u32[]{:S(2)}) %copy-start.3) | copy-done | bytes 88
  13.2 1.5 %shard_map.73 = (bf16[32,384]{1,0:T(8,128)(2,1)S(1)}, bf16[384,384]{1,0:T(8,128)(2,1)S(1)}, bf16[384,416]{1,0:T(8,128)(2,1)S(1)}, bf16[384,384]{1,0:T(8,128)(2,1)S(1)}, s32[16,128]{1,0:T(8,128)S(1)}) custom-call(s32[1,48]{1,0:T(1,128)S(1)} %bitcast.8, s32[16]{0:T(128)S(1)} %copy-done.1, s32[16]{0:T(128)S(1)} %copy-done.3, s32[192]{0:T(256)S(1)} %copy-done.2), custom_call_target="tpu_custom_call" | custom-call | flops 1000000000 | bytes 1000000 | tf_op jit(solution)/shard_map/pallas_call | solution.py:327
  14.7 8.9 %all-to-all-done = bf16[16,8,1920]{2,1,0:T(8,128)(2,1)S(1)} async-done(((bf16[16,8,1920]{2,1,0:T(8,128)(2,1)}), bf16[16,8,1920]{2,1,0:T(8,128)(2,1)S(1)}, u32[]{:S(2)}, u32[]{:S(2)}) %all-to-all-start) | async-done | bytes 491552 | tf_op jit(solution)/shard_map/all_to_all | solution.py:326
  23.6 0.2 shard_map.75
  23.8 12.5 %conditional.1 = (bf16[128,1536]{1,0:T(8,128)(2,1)S(1)}) conditional(s32[]{:T(128)} %bitcast.1, (bf16[384,384]{1,0:T(8,128)(2,1)S(1)}, s32[16,128]{1,0:T(8,128)S(1)}, bf16[128,1920]{1,0:T(8,128)(2,1)S(1)}, bf16[36,2,128,512]{3,2,1,0:T(8,128)(2,1)}, bf16[32,640]{1,0:T(8,128)(2,1)S(1)}, ...), branch_computations={%region_0.0_spmd, %region_1.0_spmd, %region_2.0_spmd, %region_3.0_... | conditional | flops 4200000000 | bytes 42043764 | solution.py:288
  24.1 0.0 copy-start.9
  24.1 1.7 %collective-permute-start.10 = (bf16[32,640]{1,0:T(8,128)(2,1)S(1)}, bf16[32,640]{1,0:T(8,128)(2,1)S(1)}, u32[]{:S(2)}, u32[]{:S(2)}) collective-permute-start(bf16[32,640]{1,0:T(8,128)(2,1)S(1)} %get-tuple-element.248), channel_id=1, source_target_pairs={{0,6},{1,7},{2,4},{3,5},{4,2},{5,3},{6,0},{7,1},{8,14},{9,15},{10,... | collective-permute-start | bytes 122888 | tf_op jit(solution)/shard_map/cond/branch_5_fun/ppermute | solution.py:282
  25.8 4.0 %branch_5_fun.4 = (bf16[192,512]{1,0:T(8,128)(2,1)S(1)}, bf16[384,640]{1,0:T(8,128)(2,1)S(1)}) custom-call(bf16[384,384]{1,0:T(8,128)(2,1)S(1)} %get-tuple-element.242.take_ref, s32[16,128]{1,0:T(8,128)S(1)} %get-tuple-element.243.limit_ref, bf16[128,1920]{1,0:T(8,128)(2,1)S(1)} %get-tuple-element.244.in_ref, ...), custom_call_target="tpu_custom_call" | custom-call | flops 2000000000 | bytes 1000000 | tf_op jit(solution)/shard_map/cond/branch_5_fun/pallas_call | solution.py:353
  29.8 0.0 collective-permute-done.10.visitor_ref
  29.8 0.0 copy-done.9
  29.8 0.7 %branch_5_fun.5.answer_ref = bf16[32,512]{1,0:T(8,128)(2,1)S(1)} custom-call(bf16[32,640]{1,0:T(8,128)(2,1)S(1)} %collective-permute-done.10.visitor_ref, s32[16,128]{1,0:T(8,128)S(1)} %get-tuple-element.243.limit_ref, bf16[36,2,128,512]{3,2,1,0:T(8,128)(2,1)S(1)} %copy-done.9), custom_call_target="tpu_custom_call" | custom-call | flops 100000000 | bytes 1000000 | tf_op jit(solution)/shard_map/cond/branch_5_fun/pallas_call | solution.py:361
  30.5 1.2 %collective-permute-start.11 = (bf16[32,512]{1,0:T(8,128)(2,1)S(1)}, bf16[32,512]{1,0:T(8,128)(2,1)S(1)}, u32[]{:S(2)}, u32[]{:S(2)}) collective-permute-start(bf16[32,512]{1,0:T(8,128)(2,1)S(1)} %branch_5_fun.5.answer_ref), channel_id=1, source_target_pairs={{0,6},{1,7},{2,4},{3,5},{4,2},{5,3},{6,0},{7,1},{8,14},{9,15},{10,... | collective-permute-start | bytes 98312 | tf_op jit(solution)/shard_map/cond/branch_5_fun/ppermute | solution.py:282
  31.7 1.6 %branch_5_fun.6.second_ref = bf16[192,512]{1,0:T(8,128)(2,1)S(1)} custom-call(bf16[384,640]{1,0:T(8,128)(2,1)S(1)} %get-tuple-element.247.rows_ref, s32[16,128]{1,0:T(8,128)S(1)} %get-tuple-element.243.limit_ref, bf16[32,512]{1,0:T(8,128)(2,1)S(1)} %branch_5_fun.5.answer_ref, bf16[36,2,128,512]{3,2,1,0:T(8,128)(2,1)S(1)} %copy-done.9), custom_call_target="tpu_custom_call" | custom-call | flops 2000000000 | bytes 1000000 | tf_op jit(solution)/shard_map/cond/branch_5_fun/pallas_call | solution.py:362
  33.3 2.1 %collective-permute-done.11.answer_ref = bf16[32,512]{1,0:T(8,128)(2,1)S(1)} collective-permute-done((bf16[32,512]{1,0:T(8,128)(2,1)S(1)}, bf16[32,512]{1,0:T(8,128)(2,1)S(1)}, u32[]{:S(2)}, u32[]{:S(2)}) %collective-permute-start.11) | collective-permute-done | bytes 32800 | tf_op jit(solution)/shard_map/cond/branch_5_fun/ppermute | solution.py:282
  35.4 0.4 branch_5_fun.7
  36.3 16.2 %all_to_all.22 = bf16[16,8,1536]{2,1,0:T(8,128)(2,1)S(1)} all-to-all(bf16[16,8,1536]{2,1,0:T(8,128)(2,1)S(1)} %bitcast.26), channel_id=1, replica_groups=mesh['groups'=2,'req'=16] {'req'}, dimensions={0} | all-to-all | bytes 786432 | tf_op jit(solution)/shard_map/all_to_all | solution.py:369
  52.5 1.1 %shard_map.76 = bf16[48,4096]{1,0:T(8,128)(2,1)} custom-call(bf16[384,384]{1,0:T(8,128)(2,1)S(1)} %get-tuple-element.326.done_ref, bf16[128,1536]{1,0:T(8,128)(2,1)S(1)} %bitcast.6), custom_call_target="tpu_custom_call" | custom-call | flops 100000000 | bytes 1000000 | tf_op jit(solution)/shard_map/pallas_call | solution.py:370
Async XLA Ops:
  2.5 21.2 %all-to-all-start = ((bf16[16,8,1920]{2,1,0:T(8,128)(2,1)}), bf16[16,8,1920]{2,1,0:T(8,128)(2,1)S(1)}, u32[]{:S(2)}, u32[]{:S(2)}) async-start(bf16[16,8,1920]{2,1,0:T(8,128)(2,1)} %bitcast.25), calls=%async_computation | async-start | bytes 983040 | tf_op jit(solution)/shard_map/all_to_all | solution.py:326
  10.5 0.7 %copy-start = (s32[48]{0:T(128)S(1)}, s32[48]{0:T(128)}, u32[]{:S(2)}) copy-start(s32[48]{0:T(128)} %param.26) | copy-start | bytes 580
  11.2 0.7 %copy-start.1 = (s32[16]{0:T(128)S(1)}, s32[16]{0:T(128)}, u32[]{:S(2)}) copy-start(s32[16]{0:T(128)} %offs_ref.3) | copy-start | bytes 196
  11.9 0.7 %copy-start.2 = (s32[192]{0:T(256)S(1)}, s32[192]{0:T(256)}, u32[]{:S(2)}) copy-start(s32[192]{0:T(256)} %lengths_ref.1) | copy-start | bytes 2308
  12.5 0.7 %copy-start.3 = (s32[16]{0:T(128)S(1)}, s32[16]{0:T(128)}, u32[]{:S(2)}) copy-start(s32[16]{0:T(128)} %moved_ref.1) | copy-start | bytes 196
  24.1 5.8 %copy-start.9 = (bf16[36,2,128,512]{3,2,1,0:T(8,128)(2,1)S(1)}, bf16[36,2,128,512]{3,2,1,0:T(8,128)(2,1)}, u32[]{:S(2)}) copy-start(bf16[36,2,128,512]{3,2,1,0:T(8,128)(2,1)} %get-tuple-element.245.cache_ref) | copy-start | bytes 28311556 | tf_op jit(solution)/shard_map/cond
  24.1 5.7 %collective-permute-start.10 = (bf16[32,640]{1,0:T(8,128)(2,1)S(1)}, bf16[32,640]{1,0:T(8,128)(2,1)S(1)}, u32[]{:S(2)}, u32[]{:S(2)}) collective-permute-start(bf16[32,640]{1,0:T(8,128)(2,1)S(1)} %get-tuple-element.248), channel_id=1, source_target_pairs={{0,6},{1,7},{2,4},{3,5},{4,2},{5,3},{6,0},{7,1},{8,14},{9,15},{10,... | collective-permute-start | bytes 122888 | tf_op jit(solution)/shard_map/cond/branch_5_fun/ppermute | solution.py:282
  30.5 4.9 %collective-permute-start.11 = (bf16[32,512]{1,0:T(8,128)(2,1)S(1)}, bf16[32,512]{1,0:T(8,128)(2,1)S(1)}, u32[]{:S(2)}, u32[]{:S(2)}) collective-permute-start(bf16[32,512]{1,0:T(8,128)(2,1)S(1)} %branch_5_fun.5.answer_ref), channel_id=1, source_target_pairs={{0,6},{1,7},{2,4},{3,5},{4,2},{5,3},{6,0},{7,1},{8,14},{9,15},{10,... | collective-permute-start | bytes 98312 | tf_op jit(solution)/shard_map/cond/branch_5_fun/ppermute | solution.py:282

commit v4 on v3

--- a/solution.py
+++ b/solution.py
@@ -21,8 +21,8 @@
 SPAN = R_DEV * GRP * DRAFT
 SLOT = GRP * DRAFT
 HALF = R_DEV // 2
-BODY = 3
-ROOM = 16
+BODY = 2
+ROOM = 48
 BF = jnp.bfloat16
 F32 = jnp.float32
 I32 = jnp.int32
@@ -65,28 +65,49 @@
     return (index >> 5) * DRAFT + (index & (DRAFT - 1)), (index >> 2) & (GRP - 1)
 
 
-def pack_kernel(count, cap, order_ref, offs_ref, rows_ref, out_ref, stack_ref):
+def pack_kernel(
+    count, cap, order_hbm, offs_hbm, rows_hbm, out_hbm, order_ref, offs_ref, rows_ref, stack_ref, pick_ref, out_ref, in_sems, out_sems
+):
+    reads = [
+        pltpu.make_async_copy(src, dst, in_sems.at[i])
+        for i, (src, dst) in enumerate([(order_hbm, order_ref), (offs_hbm, offs_ref), (rows_hbm, rows_ref)])
+    ]
+    for read in reads:
+        read.start()
     rows = rows_ref.shape[0]
+    step = 64
     me = lax.axis_index("req")
-    peer, place = peers_of(order_ref[...], offs_ref, cap, -1, me, count)
-    wide = GRP * rows
-    lane = iota((1, wide), 1)
-    part = sum([(lane >= h * rows).astype(I32) for h in range(1, GRP)])
-    tile = onehot(iota((rows, wide), 0) == lane - part * rows)
-    both = jnp.where(iota((8, rows), 0) == 0, peer, place)
-    both = exact_dot(both.astype(F32).astype(BF), tile).astype(I32)
-    spot = both[:1] * GRP + part
-    place = both[1:2]
+    gap = jnp.zeros((step - rows, WIDE), BF)
+    for h in range(GRP):
+        stack_ref[h * step + rows : (h + 1) * step, :] = gap
+    for read in reads[:2]:
+        read.wait()
+    rest = jnp.full((1, step - rows), -1, I32)
+    k = jnp.concatenate([order_ref[...], rest, order_ref[...], rest], axis=1)
+    peer, place = peers_of(k, offs_ref, cap, -1, me, count)
+    spot = peer * GRP + (iota((1, LANES), 1) >= step).astype(I32)
+    spot = jnp.where(k < 0, -1, spot + place * (count * GRP))
+    at = iota((cap * count * GRP, LANES), 0)
+    for b in range(GRP * step // LANES):
+        pick_ref[:, b * LANES : (b + 1) * LANES] = onehot(at - 2 * b == spot)
+    reads[2].wait()
     for h in range(GRP):
         for g in range(KVH):
             c = (g * GRP + h) * HD
-            stack_ref[h * rows : (h + 1) * rows, g * HD : (g + 1) * HD] = rows_ref[:, c : c + HD]
+            stack_ref[h * step : h * step + rows, g * HD : (g + 1) * HD] = rows_ref[:, c : c + HD]
         c = QW + h * HD
-        stack_ref[h * rows : (h + 1) * rows, KVH * HD :] = rows_ref[:, c : c + HD]
-    at = iota((count * GRP, wide), 0)
-    for r in range(cap):
-        here = jnp.where(place == r, spot, -1)
-        out_ref[:, r * WIDE : (r + 1) * WIDE] = exact_dot(onehot(at == here), stack_ref[...]).astype(BF)
+        stack_ref[h * step : h * step + rows, KVH * HD :] = rows_ref[:, c : c + HD]
+    writes = []
+    for start in range(0, WIDE, 2 * LANES):
+        size = min(2 * LANES, WIDE - start)
+        chunk = exact_dot(pick_ref[...], stack_ref[:, start : start + size]).astype(BF)
+        for r in range(cap):
+            cols = pl.ds(r * WIDE + start, size)
+            out_ref[:, r * WIDE + start : r * WIDE + start + size] = chunk[r * count * GRP : (r + 1) * count * GRP]
+            writes.append(pltpu.make_async_copy(out_ref.at[:, cols], out_hbm.at[:, cols], out_sems.at[len(writes)]))
+            writes[-1].start()
+    for write in writes:
+        write.wait()
 
 
 def maps_kernel(
@@ -231,30 +252,39 @@
     lax.fori_loop(0, HALF // BODY, step, 0)
 
 
-def first_kernel(count, cap, take_ref, limit_ref, in_ref, cache_ref, out_ref, rows_ref, pages_ref, sems, *scratch):
+def first_kernel(
+    count, cap, take_ref, limit_ref, in_ref, cache_ref, out_ref, rows_ref, guest_ref, later_ref, pages_ref, sems, *scratch
+):
     def fetch(s):
         return pltpu.make_async_copy(cache_ref.at[pl.ds(s * PPR, PPR)], pages_ref.at[pl.ds(s * PPR, PPR)], sems.at[s])
 
     for s in range(HALF):
         fetch(s).start()
+    moved = jnp.max(limit_ref[R_DEV : R_DEV + 1, :])
+    others = [
+        pltpu.make_async_copy(cache_ref.at[pl.ds(moved * PPR, PPR)], guest_ref, sems.at[HALF]),
+        pltpu.make_async_copy(cache_ref.at[pl.ds(HALF * PPR, HALF * PPR)], later_ref, sems.at[HALF + 1]),
+    ]
+    for other in others:
+        other.start()
     rows_ref[...] = exact_dot(take_ref[...], stacked(in_ref[...], cap)).astype(BF)
     attend_half(0, rows_ref, pages_ref, limit_ref, out_ref, scratch, lambda s: fetch(s).wait())
-
-
-def second_kernel(count, cap, rows_ref, limit_ref, answer_ref, cache_ref, out_ref, *scratch):
-    attend_half(HALF, rows_ref, cache_ref.at[pl.ds(HALF * PPR, HALF * PPR)], limit_ref, out_ref, scratch)
-
-
-def guest_kernel(count, cap, visitor_ref, limit_ref, cache_ref, out_ref, *scratch):
-    moved = jnp.max(limit_ref[R_DEV : R_DEV + 1, :])
-
+    for other in others:
+        other.wait()
+
+
+def second_kernel(count, cap, rows_ref, limit_ref, answer_ref, pages_ref, out_ref, *scratch):
+    attend_half(HALF, rows_ref, pages_ref, limit_ref, out_ref, scratch)
+
+
+def guest_kernel(count, cap, visitor_ref, limit_ref, pages_ref, out_ref, *scratch):
     def put(s, g, value):
         out_ref[:, g * HD : (g + 1) * HD] = value
 
     attend(
-        [moved],
+        [0],
         lambda s: visitor_ref[...],
-        lambda s, p, kind, cols: cache_ref[s * PPR + p, kind, :, cols],
+        lambda s, p, kind, cols: pages_ref[p, kind, :, cols],
         lambda s: limit_ref[R_DEV + 1 : R_DEV + 2, :],
         put,
         *scratch,
@@ -268,13 +298,23 @@
         out_ref[:, r * KVW : (r + 1) * KVW] = sent[r * count * GRP : (r + 1) * count * GRP]
 
 
-def finish_kernel(count, cap, done_ref, in_ref, out_ref):
+def finish_kernel(count, cap, done_ref, in_ref, out_hbm, out_ref, sems):
     rows = out_ref.shape[0]
-    result = exact_dot(done_ref[...], stacked(in_ref[...], cap)).astype(BF)
-    for h in range(GRP):
+    half = GRP // 2
+    rhs = stacked(in_ref[...], cap)
+    writes = []
+    for i in range(2):
+        result = exact_dot(done_ref[i * half * rows : (i + 1) * half * rows, :], rhs).astype(BF)
+        for h in range(half):
+            for g in range(KVH):
+                c = (g * GRP + i * half + h) * HD
+                out_ref[:, c : c + HD] = result[h * rows : (h + 1) * rows, g * HD : (g + 1) * HD]
         for g in range(KVH):
-            c = (g * GRP + h) * HD
-            out_ref[:, c : c + HD] = result[h * rows : (h + 1) * rows, g * HD : (g + 1) * HD]
+            cols = pl.ds((g * GRP + i * half) * HD, half * HD)
+            writes.append(pltpu.make_async_copy(out_ref.at[:, cols], out_hbm.at[:, cols], sems.at[i * KVH + g]))
+            writes[-1].start()
+    for write in writes:
+        write.wait()
 
 
 def through_partner(mask, count, work, *args):
@@ -306,13 +346,15 @@
     order = draft_order.reshape(1, rows)
     mask = pair_mask[0]
 
-    def call(kernel, specs, outs, scratch=(), room=8, flops=10**8):
+    anywhere = pl.BlockSpec(memory_space=pl.ANY)
+
+    def call(kernel, specs, outs, scratch=(), room=8, flops=10**8, out_spec=VMEM):
         outs = [o if isinstance(o, jax.ShapeDtypeStruct) else jax.ShapeDtypeStruct(o, BF) for o in outs]
         single = len(outs) == 1
         return pl.pallas_call(
             functools.partial(kernel, count, cap),
             in_specs=specs,
-            out_specs=VMEM if single else [VMEM] * len(outs),
+            out_specs=out_spec if single else [out_spec] * len(outs),
             out_shape=outs[0] if single else outs,
             scratch_shapes=[pltpu.VMEM(s, BF) if isinstance(s, tuple) else s for s in scratch],
             compiler_params=pltpu.CompilerParams(vmem_limit_bytes=room * 2**20),
@@ -320,9 +362,23 @@
         )
 
     wide = cap * count * GRP
-    outgoing = call(pack_kernel, [VMEM, SMEM, VMEM], [(count * GRP, cap * WIDE)], [(GRP * rows, WIDE)], room=56)(
-        order, row_offsets, draft_rows
-    )
+    outgoing = call(
+        pack_kernel,
+        [anywhere] * 3,
+        [(count * GRP, cap * WIDE)],
+        [
+            pltpu.VMEM((1, rows), I32),
+            pltpu.SMEM(row_offsets.shape, I32),
+            (rows, draft_rows.shape[1]),
+            (GRP * 64, WIDE),
+            (cap * count * GRP, GRP * 64),
+            (count * GRP, cap * WIDE),
+            pltpu.SemaphoreType.DMA((3,)),
+            pltpu.SemaphoreType.DMA((cap * pl.cdiv(WIDE, 2 * LANES),)),
+        ],
+        room=56,
+        out_spec=anywhere,
+    )(order, row_offsets, draft_rows)
     incoming = lax.all_to_all(outgoing, "req", split_axis=0, concat_axis=0, tiled=True)
     visit, take, give, done, limit = call(
         maps_kernel,
@@ -345,29 +401,34 @@
             pltpu.VMEM((slots * KVH // 2, 2 * SLOT, HD), F32),
         ]
 
-    hbm = pl.BlockSpec(memory_space=pltpu.HBM)
     pages = (HALF * PPR,) + kv_cache.shape[1:]
 
     def work(swap, visitor, take, give, limit, incoming, kv_cache):
         arrived = swap(visitor)
-        first, owned = call(
+        first, owned, guest, later = call(
             first_kernel,
-            [VMEM] * 3 + [hbm],
-            [(HALF * SLOT, KVW), (SPAN, WIDE)],
-            [pages, pltpu.SemaphoreType.DMA((HALF,))] + units(BODY),
+            [VMEM] * 3 + [anywhere],
+            [(HALF * SLOT, KVW), (SPAN, WIDE), (PPR,) + kv_cache.shape[1:], pages],
+            [pages, pltpu.SemaphoreType.DMA((HALF + 2,))] + units(BODY),
             room=ROOM,
             flops=2 * 10**9,
         )(take, limit, incoming, kv_cache)
-        answer = call(guest_kernel, [VMEM] * 3, [(SLOT, KVW)], units(1), room=16)(arrived, limit, kv_cache)
+        answer = call(guest_kernel, [VMEM] * 3, [(SLOT, KVW)], units(1), room=8)(arrived, limit, guest)
         second = call(
-            second_kernel, [VMEM] * 4, [(HALF * SLOT, KVW)], units(BODY), room=16, flops=2 * 10**9
-        )(owned, limit, answer, kv_cache)
+            second_kernel, [VMEM] * 4, [(HALF * SLOT, KVW)], units(BODY), room=8, flops=2 * 10**9
+        )(owned, limit, answer, later)
         answer = swap(answer)
         return call(reply_kernel, [VMEM] * 4, [(count * GRP, cap * KVW)])(give, first, second, answer)
 
     backward = through_partner(mask, count, work, visitor, take, give, limit, incoming, kv_cache)
     returned = lax.all_to_all(backward, "req", split_axis=0, concat_axis=0, tiled=True)
-    return call(finish_kernel, [VMEM] * 2, [(rows, QW)])(done, returned)
+    return call(
+        finish_kernel,
+        [VMEM] * 2,
+        [(rows, QW)],
+        [(rows, QW), pltpu.SemaphoreType.DMA((2 * KVH,))],
+        out_spec=anywhere,
+    )(done, returned)
 
 
 def solution(mesh):

time: 52.7 us -> 52.4 us (level)
  waiting for transfers between devices: 11 us -> 9.77 us
  blocking collectives: 16.2 us -> 17 us
    ppermute x2, waiting for transfers between devices: 2.13 us -> 0.88 us  [permuted(): return lax.ppermute(value, 'req', [(i, i ^ by) for i in range(count)])]
    all_to_all x1, blocking collectives: 16.2 us -> 17 us  [on_device(): lax.all_to_all(backward, 'req', split_axis=0, concat_axis=0, tiled=True)]
  transfers between devices with their start and end apart: 3 -> 3, of which waited for: 2 -> 2; matrix products, arithmetic and copies ran while one was open for 0% -> 0% of each run, Pallas kernels for 13% -> 14%
where the time goes in v4:
time: 52.4 us; the launch traced here: 53.3 us
  blocking collectives  17 us (32%)
  Pallas kernels  12.1 us (23%)
  starting transfers between devices  10.2 us (19%)
  waiting for transfers between devices  9.77 us (19%)
  local copies, waits for them, and re-layouts  2.64 us (5%)
  between operations  0.92 us (2%)
  loops' own time  0.61 us (1%)
    all_to_all x1, blocking collectives, on_device(): lax.all_to_all(backward, 'req', split_axis=0, concat_axis=0, tiled=True)  17 us
    all_to_all x1, waiting for transfers between devices, on_device(): lax.all_to_all(outgoing, 'req', split_axis=0, concat_axis=0, tiled=True)  8.89 us
    all_to_all x1, starting transfers between devices, on_device(): lax.all_to_all(outgoing, 'req', split_axis=0, concat_axis=0, tiled=True)  7.4 us
    pallas_call x1, Pallas kernels, work(): call(first_kernel, [VMEM] * 3 + [anywhere], [(HALF * SLOT, KVW), (SPAN, W...  4.17 us
    ppermute x2, starting transfers between devices, permuted(): return lax.ppermute(value, 'req', [(i, i ^ by) for i in range(count)])  2.78 us
    unnamed x8, local copies, waits for them, and re-layouts  2.64 us
    pallas_call x1, Pallas kernels, on_device(): call(pack_kernel, [anywhere] * 3, [(count * GRP, cap * WIDE)], [pltpu.VME...  2.33 us
    pallas_call x1, Pallas kernels, work(): call(second_kernel, [VMEM] * 4, [(HALF * SLOT, KVW)], units(BODY), room=8...  1.95 us
  transfers between devices with their start and end apart: 3, of which 2 were waited for; matrix products, arithmetic and copies ran while one was open for 0% of the time, Pallas kernels for 14%

profile of v4, /device:TPU:0, one launch (start us, length us, event | category | flops | bytes accessed | tf_op | source)
XLA Modules:
  0.0 53.3 jit_solution(7691887313658658608)
XLA Ops:
  0.0 2.3 %shard_map.74 = bf16[128,1920]{1,0:T(8,128)(2,1)} custom-call(s32[1,48]{1,0:T(1,128)} %bitcast.7, s32[16]{0:T(128)} %offs_hbm.1, bf16[48,5120]{1,0:T(8,128)(2,1)} %rows_hbm.1), custom_call_target="tpu_custom_call" | custom-call | flops 100000000 | bytes 1000000 | tf_op jit(solution)/shard_map/pallas_call | solution.py:365
  2.3 7.4 %all-to-all-start = ((bf16[16,8,1920]{2,1,0:T(8,128)(2,1)}), bf16[16,8,1920]{2,1,0:T(8,128)(2,1)S(1)}, u32[]{:S(2)}, u32[]{:S(2)}) async-start(bf16[16,8,1920]{2,1,0:T(8,128)(2,1)} %bitcast.25), calls=%async_computation | async-start | bytes 983040 | tf_op jit(solution)/shard_map/all_to_all | solution.py:382
  10.4 0.0 copy-start
  10.4 0.6 %copy-done = s32[48]{0:T(128)S(1)} copy-done((s32[48]{0:T(128)S(1)}, s32[48]{0:T(128)}, u32[]{:S(2)}) %copy-start) | copy-done | bytes 216
  11.1 0.0 copy-start.1
  11.1 0.7 %copy-done.1 = s32[16]{0:T(128)S(1)} copy-done((s32[16]{0:T(128)S(1)}, s32[16]{0:T(128)}, u32[]{:S(2)}) %copy-start.1) | copy-done | bytes 88
  11.7 0.0 copy-start.2
  11.7 0.7 %copy-done.2 = s32[192]{0:T(256)S(1)} copy-done((s32[192]{0:T(256)S(1)}, s32[192]{0:T(256)}, u32[]{:S(2)}) %copy-start.2) | copy-done | bytes 792
  12.4 0.0 copy-start.3
  12.4 0.7 %copy-done.3 = s32[16]{0:T(128)S(1)} copy-done((s32[16]{0:T(128)S(1)}, s32[16]{0:T(128)}, u32[]{:S(2)}) %copy-start.3) | copy-done | bytes 88
  13.0 1.5 %shard_map.73 = (bf16[32,384]{1,0:T(8,128)(2,1)S(1)}, bf16[384,384]{1,0:T(8,128)(2,1)S(1)}, bf16[384,416]{1,0:T(8,128)(2,1)S(1)}, bf16[384,384]{1,0:T(8,128)(2,1)S(1)}, s32[16,128]{1,0:T(8,128)S(1)}) custom-call(s32[1,48]{1,0:T(1,128)S(1)} %bitcast.8, s32[16]{0:T(128)S(1)} %copy-done.1, s32[16]{0:T(128)S(1)} %copy-done.3, s32[192]{0:T(256)S(1)} %copy-done.2), custom_call_target="tpu_custom_call" | custom-call | flops 1000000000 | bytes 1000000 | tf_op jit(solution)/shard_map/pallas_call | solution.py:383
  14.6 8.9 %all-to-all-done = bf16[16,8,1920]{2,1,0:T(8,128)(2,1)S(1)} async-done(((bf16[16,8,1920]{2,1,0:T(8,128)(2,1)}), bf16[16,8,1920]{2,1,0:T(8,128)(2,1)S(1)}, u32[]{:S(2)}, u32[]{:S(2)}) %all-to-all-start) | async-done | bytes 491552 | tf_op jit(solution)/shard_map/all_to_all | solution.py:382
  23.5 0.2 shard_map.75
  23.7 11.2 %conditional.1 = (bf16[128,1536]{1,0:T(8,128)(2,1)S(1)}) conditional(s32[]{:T(128)} %bitcast.1, (bf16[384,384]{1,0:T(8,128)(2,1)S(1)}, s32[16,128]{1,0:T(8,128)S(1)}, bf16[128,1920]{1,0:T(8,128)(2,1)S(1)}, bf16[36,2,128,512]{3,2,1,0:T(8,128)(2,1)}, bf16[32,640]{1,0:T(8,128)(2,1)S(1)}, ...), branch_computations={%region_0.0_spmd, %region_1.0_spmd, %region_2.0_spmd, %region_3.0_... | conditional | flops 4200000000 | bytes 4295000 | solution.py:328
  23.9 1.3 %collective-permute-start.16 = (bf16[32,640]{1,0:T(8,128)(2,1)S(1)}, bf16[32,640]{1,0:T(8,128)(2,1)S(1)}, u32[]{:S(2)}, u32[]{:S(2)}) collective-permute-start(bf16[32,640]{1,0:T(8,128)(2,1)S(1)} %get-tuple-element.288), channel_id=1, source_target_pairs={{0,9},{1,8},{2,11},{3,10},{4,13},{5,12},{6,15},{7,14},{8,1},{9,0},... | collective-permute-start | bytes 122888 | tf_op jit(solution)/shard_map/cond/branch_8_fun/ppermute | solution.py:322
  25.3 4.2 %branch_8_fun.4 = (bf16[192,512]{1,0:T(8,128)(2,1)S(1)}, bf16[384,640]{1,0:T(8,128)(2,1)S(1)}, bf16[3,2,128,512]{3,2,1,0:T(8,128)(2,1)S(1)}, bf16[18,2,128,512]{3,2,1,0:T(8,128)(2,1)S(1)}) custom-call(bf16[384,384]{1,0:T(8,128)(2,1)S(1)} %get-tuple-element.282.take_ref, s32[16,128]{1,0:T(8,128)S(1)} %get-tuple-element.283.limit_ref, ...), custom_call_target="tpu_custom_call" | custom-call | flops 2000000000 | bytes 1000000 | tf_op jit(solution)/shard_map/cond/branch_8_fun/pallas_call | solution.py:408
  29.4 0.0 collective-permute-done.16.visitor_ref
  29.4 0.5 branch_8_fun.5.answer_ref
  29.9 1.5 %collective-permute-start.17 = (bf16[32,512]{1,0:T(8,128)(2,1)S(1)}, bf16[32,512]{1,0:T(8,128)(2,1)S(1)}, u32[]{:S(2)}, u32[]{:S(2)}) collective-permute-start(bf16[32,512]{1,0:T(8,128)(2,1)S(1)} %branch_8_fun.5.answer_ref), channel_id=1, source_target_pairs={{0,9},{1,8},{2,11},{3,10},{4,13},{5,12},{6,15},{7,14},{8,1},{9,0},... | collective-permute-start | bytes 98312 | tf_op jit(solution)/shard_map/cond/branch_8_fun/ppermute | solution.py:322
  31.4 1.9 %branch_8_fun.6.second_ref = bf16[192,512]{1,0:T(8,128)(2,1)S(1)} custom-call(bf16[384,640]{1,0:T(8,128)(2,1)S(1)} %get-tuple-element.287.rows_ref, s32[16,128]{1,0:T(8,128)S(1)} %get-tuple-element.283.limit_ref, bf16[32,512]{1,0:T(8,128)(2,1)S(1)} %branch_8_fun.5.answer_ref, bf16[18,2,128,512]{3,2,1,0:T(8,128)(2,1)S(1)} %get-tuple-element.290.pages_ref), custom_call_target="tpu_custom_call" | custom-call | flops 2000000000 | bytes 1000000 | tf_op jit(solution)/shard_map/cond/branch_8_fun/pallas_call | solution.py:417
  33.4 0.9 %collective-permute-done.17.answer_ref = bf16[32,512]{1,0:T(8,128)(2,1)S(1)} collective-permute-done((bf16[32,512]{1,0:T(8,128)(2,1)S(1)}, bf16[32,512]{1,0:T(8,128)(2,1)S(1)}, u32[]{:S(2)}, u32[]{:S(2)}) %collective-permute-start.17) | collective-permute-done | bytes 32800 | tf_op jit(solution)/shard_map/cond/branch_8_fun/ppermute | solution.py:322
  34.2 0.4 branch_8_fun.7
  34.9 17.0 %all_to_all.22 = bf16[16,8,1536]{2,1,0:T(8,128)(2,1)S(1)} all-to-all(bf16[16,8,1536]{2,1,0:T(8,128)(2,1)S(1)} %bitcast.26), channel_id=1, replica_groups=mesh['groups'=2,'req'=16] {'req'}, dimensions={0} | all-to-all | bytes 786432 | tf_op jit(solution)/shard_map/all_to_all | solution.py:424
  52.0 1.1 %shard_map.76 = bf16[48,4096]{1,0:T(8,128)(2,1)} custom-call(bf16[384,384]{1,0:T(8,128)(2,1)S(1)} %get-tuple-element.356.done_ref, bf16[128,1536]{1,0:T(8,128)(2,1)S(1)} %bitcast.6), custom_call_target="tpu_custom_call" | custom-call | flops 100000000 | bytes 1000000 | tf_op jit(solution)/shard_map/pallas_call | solution.py:425
Async XLA Ops:
  2.3 21.1 %all-to-all-start = ((bf16[16,8,1920]{2,1,0:T(8,128)(2,1)}), bf16[16,8,1920]{2,1,0:T(8,128)(2,1)S(1)}, u32[]{:S(2)}, u32[]{:S(2)}) async-start(bf16[16,8,1920]{2,1,0:T(8,128)(2,1)} %bitcast.25), calls=%async_computation | async-start | bytes 983040 | tf_op jit(solution)/shard_map/all_to_all | solution.py:382
  10.4 0.7 %copy-start = (s32[48]{0:T(128)S(1)}, s32[48]{0:T(128)}, u32[]{:S(2)}) copy-start(s32[48]{0:T(128)} %param.26) | copy-start | bytes 580
  11.1 0.7 %copy-start.1 = (s32[16]{0:T(128)S(1)}, s32[16]{0:T(128)}, u32[]{:S(2)}) copy-start(s32[16]{0:T(128)} %offs_hbm.1) | copy-start | bytes 196
  11.7 0.7 %copy-start.2 = (s32[192]{0:T(256)S(1)}, s32[192]{0:T(256)}, u32[]{:S(2)}) copy-start(s32[192]{0:T(256)} %lengths_ref.1) | copy-start | bytes 2308
  12.4 0.7 %copy-start.3 = (s32[16]{0:T(128)S(1)}, s32[16]{0:T(128)}, u32[]{:S(2)}) copy-start(s32[16]{0:T(128)} %moved_ref.1) | copy-start | bytes 196
  23.9 5.5 %collective-permute-start.16 = (bf16[32,640]{1,0:T(8,128)(2,1)S(1)}, bf16[32,640]{1,0:T(8,128)(2,1)S(1)}, u32[]{:S(2)}, u32[]{:S(2)}) collective-permute-start(bf16[32,640]{1,0:T(8,128)(2,1)S(1)} %get-tuple-element.288), channel_id=1, source_target_pairs={{0,9},{1,8},{2,11},{3,10},{4,13},{5,12},{6,15},{7,14},{8,1},{9,0},... | collective-permute-start | bytes 122888 | tf_op jit(solution)/shard_map/cond/branch_8_fun/ppermute | solution.py:322
  29.9 4.3 %collective-permute-start.17 = (bf16[32,512]{1,0:T(8,128)(2,1)S(1)}, bf16[32,512]{1,0:T(8,128)(2,1)S(1)}, u32[]{:S(2)}, u32[]{:S(2)}) collective-permute-start(bf16[32,512]{1,0:T(8,128)(2,1)S(1)} %branch_8_fun.5.answer_ref), channel_id=1, source_target_pairs={{0,9},{1,8},{2,11},{3,10},{4,13},{5,12},{6,15},{7,14},{8,1},{9,0},... | collective-permute-start | bytes 98312 | tf_op jit(solution)/shard_map/cond/branch_8_fun/ppermute | solution.py:322
